TPU v7x, 32 devices: a whole 2x2x4 slice. The times are simulated.
32 devices in a mesh: dp: 4 (over y, core), seq: 8 (over z, x).
Axes of the slice: x: 2, y: 2, z: 4, core: 2. Of those that a mesh axis runs over, the one named last changes fastest.
Arguments:
- inputs: bfloat16 [4096, 768], P(('dp', 'seq')), may hold values from -6 to 6
- norm_gain: float32 [768], replicated, may hold values from 0.5 to 1.5
- in_proj: bfloat16 [768, 3352], P(('dp', 'seq')), may hold values from -0.21875 to 0.21875
- conv_weight: float32 [1792, 4], replicated, may hold values from -0.5 to 0.5
- conv_bias: float32 [1792], replicated, may hold values from -0.5 to 0.5
- dt_bias: float32 [24], replicated, may hold values from -10 to -3
- a_log: float32 [24], replicated, may hold values from -1 to 1.5
- skip_gain: float32 [24], replicated, may hold values from 0.5 to 1.5
- gated_gain: float32 [1536], replicated, may hold values from 0.5 to 1.5
- out_proj: bfloat16 [768, 1536], P(('dp', 'seq')), may hold values from -0.15625 to 0.15625
- cotangent: bfloat16 [4096, 768], P(('dp', 'seq')), may hold values from -6 to 6
Outputs:
- layer_out: bfloat16 [4096, 768], P(('dp', 'seq'))
- input_grad: float32 [4096, 768], P(('dp', 'seq'))
- in_proj_grad: float32 [768, 3352], P(('dp', 'seq'))
- out_proj_grad: float32 [768, 1536], P(('dp', 'seq'))
- norm_gain_grad: float32 [768], replicated
- conv_weight_grad: float32 [1792, 4], replicated
- conv_bias_grad: float32 [1792], replicated
- dt_bias_grad: float32 [24], replicated
- a_log_grad: float32 [24], replicated
- skip_grad: float32 [24], replicated
- gated_gain_grad: float32 [1536], replicated
All inputs are finite; a program needn't handle non-finite values.
Results may differ from a plain program's by a relative error of at most 0.015.
Values may be sent and summed in bfloat16 or wider, within the bound.
A program may use at most 192 MiB of HBM per device.

v0:
```python
from functools import partial

import jax
import jax.numpy as jnp
from jax import lax
from jax.sharding import PartitionSpec as P

HEADS = 24
HEAD_DIM = 64
STATE = 128
CONV = 4
DI = 1536
XBC = 1792


EPS = 1e-05
HIGH = lax.Precision.HIGHEST


def passed_along(value, axis, steps):
    count = lax.axis_size(axis)
    first, last = (max(0, -steps), min(count, count - steps))
    return lax.ppermute(value, axis, [(source, source + steps) for source in range(first, last)])


def prefix(shard, axis, join, neutral):
    place = lax.axis_index(axis)
    gathered = jax.tree.map(
        lambda a, kind: lax.all_gather(a.astype(kind), axis), shard, (jnp.bfloat16, jnp.bfloat16)
    )
    state = jax.tree.map(lambda a, e: jnp.zeros_like(a) + jnp.asarray(e, a.dtype), shard, neutral)

    def one(hop, state):
        return join(
            state,
            jax.tree.map(
                lambda a, own: lax.dynamic_index_in_dim(a, hop, 0, False).astype(own.dtype),
                gathered,
                shard,
            ),
        )

    return lax.fori_loop(0, place, one, state)


def prefix_2(shard, axis, join, neutral):
    count = lax.axis_size(axis)
    place = lax.axis_index(axis)
    ahead = count - 1 - place
    gathered = jax.tree.map(
        lambda a, kind: lax.all_gather(a.astype(kind), axis),
        shard,
        jax.tree.map(lambda a: jnp.bfloat16 if a.dtype == jnp.float32 else a.dtype, shard),
    )
    state = jax.tree.map(lambda a, e: jnp.zeros_like(a) + jnp.asarray(e, a.dtype), shard, neutral)

    def one(hop, state):
        source = count - 1 - hop
        return join(
            state,
            jax.tree.map(
                lambda a, own: lax.dynamic_index_in_dim(a, source, 0, False).astype(own.dtype),
                gathered,
                shard,
            ),
        )

    return lax.fori_loop(0, ahead, one, state)


def pre_norm(residual_in, norm_gain):
    scale_rms = lax.rsqrt(jnp.mean(residual_in * residual_in, axis=-1, keepdims=True) + EPS)
    return residual_in * scale_rms * norm_gain


def conv_silu(padded, conv_weight, conv_bias, row_count):
    total = jnp.zeros((row_count, padded.shape[1]), jnp.float32) + conv_bias[None, :]
    for offset in range(conv_weight.shape[1]):
        total = total + conv_weight[:, offset][None, :] * padded[offset : offset + row_count]
    return jax.nn.silu(total)


def ssd_block(heads_x, b_block, c_block, step_block, decay_block, carried):
    cumulative = jnp.cumsum(decay_block, axis=0)
    by_head = cumulative.T
    spread = by_head[:, :, None] - by_head[:, None, :]
    places = jnp.arange(decay_block.shape[0])
    lower = places[:, None] >= places[None, :]
    weights_mat = jnp.exp(jnp.where(lower[None], spread, -jnp.inf))
    intersection = jnp.dot(c_block, b_block.T, precision=HIGH)
    scaled_x = heads_x * step_block[:, :, None]
    scores = weights_mat * intersection[None]
    output = jnp.einsum("hts,shp->thp", scores, scaled_x, precision=HIGH)
    output = (
        output
        + jnp.einsum("tn,hpn->thp", c_block, carried, precision=HIGH)
        * jnp.exp(cumulative)[:, :, None]
    )
    tail = jnp.exp(cumulative[-1][None, :] - cumulative)
    fresh = jnp.einsum("shp,sn->hpn", scaled_x * tail[:, :, None], b_block, precision=HIGH)
    return (output, fresh + jnp.exp(cumulative[-1])[:, None, None] * carried)


def ssd_scan(xs, b_mat, c_mat, step, log_decay, block_rows):
    row_count = xs.shape[0]
    count = row_count // block_rows
    pieces = (
        xs.reshape(count, block_rows, HEADS, HEAD_DIM),
        b_mat.reshape(count, block_rows, STATE),
        c_mat.reshape(count, block_rows, STATE),
        step.reshape(count, block_rows, HEADS),
        log_decay.reshape(count, block_rows, HEADS),
    )
    start_state = jnp.zeros((HEADS, HEAD_DIM, STATE), jnp.float32)

    def advance(carried, piece):
        output, carried = ssd_block(piece[0], piece[1], piece[2], piece[3], piece[4], carried)
        return (carried, output)

    final, outputs = lax.scan(advance, start_state, pieces)
    return (outputs.reshape(row_count, HEADS * HEAD_DIM), final)


def mid_local(xbc, dt_raw, edge, conv_weight, conv_bias, dt_bias, a_log, block_rows):
    row_count = xbc.shape[0]
    activated = conv_silu(jnp.concatenate([edge, xbc], axis=0), conv_weight, conv_bias, row_count)
    xs = activated[:, :DI]
    b_mat = activated[:, DI : DI + STATE]
    c_mat = activated[:, DI + STATE :]
    step = jax.nn.softplus(dt_raw + dt_bias)
    log_decay = step * -jnp.exp(a_log)
    ssd_out, final = ssd_scan(xs, b_mat, c_mat, step, log_decay, block_rows)
    return (ssd_out, xs, c_mat, jnp.cumsum(log_decay, axis=0), final)


def post_gate(ssd_out, xs, gate_part, skip_gain, gated_gain):
    row_count = xs.shape[0]
    skipped = (xs.reshape(row_count, HEADS, HEAD_DIM) * skip_gain[None, :, None]).reshape(
        row_count, DI
    )
    mixed_in = (ssd_out + skipped) * jax.nn.silu(gate_part)
    scale_rms = lax.rsqrt(jnp.mean(mixed_in * mixed_in, axis=-1, keepdims=True) + EPS)
    return mixed_in * scale_rms * gated_gain


def forward_chain(earlier, later):
    return (earlier[0] * later[0], later[0][:, None, None] * earlier[1] + later[1])


def reverse_chain(earlier, later):
    return (earlier[0] * later[0], later[1] + later[0][:, None, None] * earlier[1])


def contract_rows(left, right):
    return lax.dot_general(
        left, right, (((0,), (0,)), ((), ())), preferred_element_type=jnp.float32
    )


def contract_cols(left, right):
    return lax.dot_general(
        left, right, (((1,), (1,)), ((), ())), preferred_element_type=jnp.float32
    )


def owner_rows(count, per_device, groups, seq_count):
    places = jnp.arange(count, dtype=jnp.int32)
    seq_index = places // (groups * per_device)
    within = places % (groups * per_device)
    group_index = within // per_device
    return (group_index * seq_count + seq_index) * per_device + within % per_device


def body(
    inputs,
    norm_gain,
    in_proj,
    conv_weight,
    conv_bias,
    dt_bias,
    a_log,
    skip_gain,
    gated_gain,
    out_proj,
    cotangent,
):
    row_count = inputs.shape[0]
    residual_in = inputs.astype(jnp.float32)
    normed_full, norm_back = jax.vjp(pre_norm, residual_in, norm_gain)
    normed = normed_full.astype(jnp.bfloat16)
    columns = normed
    projected = jnp.dot(
        columns,
        lax.all_gather(in_proj, ("dp", "seq"), axis=0, tiled=True),
        preferred_element_type=jnp.float32,
    )
    gate_part = projected[:, :DI]
    xbc = projected[:, DI : DI + XBC]
    dt_raw = projected[:, DI + XBC :]
    edge = passed_along(xbc[row_count - (CONV - 1) :], "seq", 1)
    primal, mid_back = jax.vjp(
        partial(mid_local, block_rows=row_count),
        xbc,
        dt_raw,
        edge,
        conv_weight,
        conv_bias,
        dt_bias,
        a_log,
    )
    local_out, xs, c_mat, cumulative, s_local = primal
    decay = jnp.exp(cumulative[-1])
    identity = (jnp.ones((HEADS,), jnp.float32), jnp.zeros((HEADS, HEAD_DIM, STATE), jnp.float32))
    scanned = prefix((decay, s_local), "seq", forward_chain, identity)
    state_in = scanned[1]
    weighted = jnp.exp(cumulative)
    carried_part = jnp.einsum("tn,hpn->thp", c_mat, state_in, precision=HIGH) * weighted[:, :, None]
    ssd_out = local_out + carried_part.reshape(row_count, DI)
    gated_full, post_back = jax.vjp(post_gate, ssd_out, xs, gate_part, skip_gain, gated_gain)
    gated = gated_full.astype(jnp.bfloat16)
    mixed = contract_cols(gated, lax.all_gather(out_proj, ("dp", "seq"), axis=0, tiled=True))
    layer_out = (residual_in + mixed).astype(jnp.bfloat16)
    columns = cotangent
    gated_cot = jnp.dot(
        columns,
        lax.all_gather(out_proj, ("dp", "seq"), axis=0, tiled=True),
        preferred_element_type=jnp.float32,
    )
    ssd_cot, xs_cot, gate_cot, skip_grad, gated_gain_grad = post_back(gated_cot)
    ssd_heads = ssd_cot.reshape(row_count, HEADS, HEAD_DIM)
    scaled_cot = ssd_heads * weighted[:, :, None]
    local_grad = jnp.einsum("thp,tn->hpn", scaled_cot, c_mat, precision=HIGH)
    later_grad = prefix_2((decay, local_grad), "seq", reverse_chain, identity)[1]
    c_cot = jnp.einsum("thp,hpn->tn", scaled_cot, state_in, precision=HIGH)
    cum_cot = jnp.sum(ssd_heads * carried_part, axis=2)
    cum_cot = cum_cot.at[-1].add(jnp.sum(later_grad * state_in, axis=(1, 2)) * decay)
    mid_grads = mid_back((ssd_cot, xs_cot, c_cot, cum_cot, later_grad))
    xbc_cot, dt_cot, edge_cot, conv_weight_grad, conv_bias_grad, dt_bias_grad, a_log_grad = (
        mid_grads
    )
    edge_back = passed_along(edge_cot, "seq", -1)
    xbc_cot = xbc_cot.at[row_count - (CONV - 1) :].add(edge_back)
    projected_cot = jnp.concatenate([gate_cot, xbc_cot, dt_cot], axis=1).astype(jnp.bfloat16)
    per_device = in_proj.shape[0]
    groups = lax.axis_size("dp")
    seq_count = lax.axis_size("seq")
    picked = owner_rows(groups * per_device * lax.axis_size("seq"), per_device, groups, seq_count)
    in_section = lax.psum_scatter(
        contract_rows(jnp.take(normed, picked, axis=1), projected_cot).astype(jnp.bfloat16),
        "seq",
        scatter_dimension=0,
        tiled=True,
    )
    picked = owner_rows(groups * per_device * lax.axis_size("seq"), per_device, groups, seq_count)
    out_section = lax.psum_scatter(
        contract_rows(jnp.take(cotangent, picked, axis=1), gated).astype(jnp.bfloat16),
        "seq",
        scatter_dimension=0,
        tiled=True,
    )
    in_proj_grad, out_proj_grad = (
        lax.psum_scatter(in_section, "dp", scatter_dimension=0, tiled=True).astype(jnp.float32),
        lax.psum_scatter(out_section, "dp", scatter_dimension=0, tiled=True).astype(jnp.float32),
    )
    normed_cot = contract_cols(
        projected_cot, lax.all_gather(in_proj, ("dp", "seq"), axis=0, tiled=True)
    )
    input_part, norm_gain_grad = norm_back(normed_cot)
    input_grad = cotangent.astype(jnp.float32) + input_part
    summed = lax.psum(
        (
            norm_gain_grad,
            conv_weight_grad,
            conv_bias_grad,
            dt_bias_grad,
            a_log_grad,
            skip_grad,
            gated_gain_grad,
        ),
        ("dp", "seq"),
    )
    return (
        layer_out,
        input_grad,
        in_proj_grad,
        out_proj_grad,
        summed[0],
        summed[1],
        summed[2],
        summed[3],
        summed[4],
        summed[5],
        summed[6],
    )


def solution(mesh):
    placed = (
        P(("dp", "seq"), None),
        P(),
        P(("dp", "seq"), None),
        P(),
        P(),
        P(),
        P(),
        P(),
        P(),
        P(("dp", "seq"), None),
        P(("dp", "seq"), None),
    )
    return jax.shard_map(
        body,
        mesh=mesh,
        in_specs=placed,
        out_specs=(
            P(("dp", "seq"), None),
            P(("dp", "seq"), None),
            P(("dp", "seq"), None),
            P(("dp", "seq"), None),
            P(),
            P(),
            P(),
            P(),
            P(),
            P(),
            P(),
        ),
        check_vma=False,
    )
```

profile of v0, /device:TPU:0, one launch (start us, length us, event | category | flops | bytes accessed | tf_op | source)
XLA Modules:
  0.0 567.7 jit_solution(5006229318073600678)
XLA Ops:
  12.3 66.9 %all-gather.8.cloned.1.call-done = bf16[768,3352]{1,0:T(8,128)(2,1)} async-done(((bf16[24,3352]{1,0:T(8,128)(2,1)}), bf16[768,3352]{1,0:T(8,128)(2,1)}) %all-gather.8.cloned.1.call-update) | async-done | bytes 5148688 | tf_op jit(solution)/shard_map/all_gather | solution.py:194
  79.2 4.7 fusion.145
  85.6 3.3 collective-permute-start
  90.5 1.3 copy.160
  91.8 6.7 %fusion.31 = (f32[128,1792]{0,1:T(8,128)S(1)}, f32[128,1792]{0,1:T(8,128)}) fusion(f32[128,1792]{0,1:T(8,128)} %slice.108, f32[1792]{0:T(1024)S(1)} %get-tuple-element.342, f32[3,1792]{0,1:T(8,128)} %copy.160, f32[1792]{0:T(1024)S(1)} %get-tuple-element.343, f32[1792]{0:T(1024)S(1)} %get-tuple-element.341, f32[1792]{0:T(1024)S(1)} %get-tuple-element.340, ...), kind=kLoop, calls=%fused_computation.52 | loop fusion | flops 3440640 | bytes 2809856 | tf_op jit(solution)/shard_map/jvp(jit(silu))/mul | solution.py:80
  99.4 1.5 fusion.20
  102.2 2.5 gather_fusion.1
  106.1 20.2 %all-gather.2 = bf16[8,1,24]{2,1,0:T(2,128)(2,1)S(1)} all-gather(bf16[1,1,24]{2,1,0:T(2,128)(2,1)S(1)} %bitcast.120), channel_id=1, replica_groups=mesh['dp'=4,'seq'=8] {'seq'}, dimensions={0}, use_global_device_ids=true | all-gather | bytes 432 | tf_op jit(solution)/shard_map/all_gather | solution.py:29
  127.3 1.6 fusion.70
  129.0 32.5 %all-gather.12.cloned.1.call-done = bf16[192,64,128]{2,1,0:T(8,128)(2,1)} async-done(((bf16[24,64,128]{2,1,0:T(8,128)(2,1)}), bf16[192,64,128]{2,1,0:T(8,128)(2,1)}) %all-gather.12.cloned.1.call-update) | async-done | bytes 3145744 | tf_op jit(solution)/shard_map/all_gather | solution.py:29
  163.2 4.2 fusion.17
  168.8 2.3 convolution_convert_fusion.1
  171.1 49.1 %all-gather.10.cloned.1.call-done = bf16[768,1536]{1,0:T(8,128)(2,1)} async-done(((bf16[24,1536]{1,0:T(8,128)(2,1)}), bf16[768,1536]{1,0:T(8,128)(2,1)}) %all-gather.10.cloned.1.call-update) | async-done | bytes 2359312 | tf_op jit(solution)/shard_map/all_gather | solution.py:221
  220.3 3.7 multiply_reduce_fusion.5
  224.0 3.4 multiply_reduce_fusion.6
  227.5 1.5 convolution_convert_fusion.2
  229.5 2.5 gather_fusion
  232.0 2.2 multiply_reduce_fusion.7
  234.2 4.1 fusion.26
  241.4 1.4 fusion.22
  242.9 49.1 %reduce-scatter.9.cloned.1.call-done = bf16[96,1536]{1,0:T(8,128)(2,1)} async-done(((bf16[768,1536]{1,0:T(8,128)(2,1)}), bf16[96,1536]{1,0:T(8,128)(2,1)}) %reduce-scatter.9.cloned.1.call-update) | async-done | bytes 294928 | tf_op jit(solution)/shard_map/reduce_scatter | solution.py:255
  292.1 61.2 %all-gather.14.cloned.1.call-done = bf16[192,64,128]{2,1,0:T(8,128)(2,1)} async-done(((bf16[24,64,128]{2,1,0:T(8,128)(2,1)}), bf16[192,64,128]{2,1,0:T(8,128)(2,1)}) %all-gather.14.cloned.1.call-update) | async-done | bytes 3145744 | tf_op jit(solution)/shard_map/all_gather | solution.py:51
  353.4 13.4 %while.19 = (s32[]{:T(128)}, f32[24,64,128]{2,1,0:T(8,128)S(1)}, s32[]{:T(128)}, bf16[8,24,64,128]{3,2,1,0:T(8,128)(2,1)}, bf16[8,24]{1,0:T(8,128)(2,1)}, /*index=5*/s32[]{:T(128)}, s32[]{:T(128)}, s32[]{:T(128)}, s32[]{:T(128)}) while((s32[]{:T(128)}, f32[24,64,128]{2,1,0:T(8,128)S(1)}, s32[]{:T(128)}, bf16[8,24,64,128]{3,2,1,0:T(8,128)(2,1)}, ...), condition=%wide.region_8.9_spmd, body=%wide.region_7.8_spmd.sunk | while | flops 589854 | bytes 1966475 | solution.py:68
  354.1 1.2 convert_add_fusion.5
  356.0 1.2 convert_add_fusion.5
  357.9 1.2 convert_add_fusion.5
  359.8 1.2 convert_add_fusion.5
  361.8 1.2 convert_add_fusion.5
  363.7 1.2 convert_add_fusion.5
  365.6 1.2 convert_add_fusion.5
  367.1 1.6 fusion.86
  368.7 1.4 fusion.24
  370.1 2.5 multiply_reduce_fusion.8
  378.7 6.3 %multiply_reduce_fusion.3 = (f32[1792]{0:T(1024)}, f32[1792]{0:T(1024)}, f32[1792]{0:T(1024)}, f32[1792]{0:T(1024)}, f32[1792]{0:T(1024)}, /*index=5*/f32[128,1792]{0,1:T(8,128)S(1)}) fusion(f32[128,1792]{0,1:T(8,128)} %slice.108, f32[3,1792]{0,1:T(8,128)} %copy.160, f32[128,3352]{0,1:T(8,128)S(1)} %copy-done.1, f32[128,1792]{0,1:T(8,128)} %get-tuple-element.379, ...), kind=kLoop, calls=%fused_computation.49 | loop fusion | flops 5266688 | bytes 4644864 | tf_op jit(solution)/shard_map/transpose(jvp())/reduce_sum | solution.py:79
  385.0 1.3 broadcast_multiply_fusion
  386.3 1.5 pad_add_fusion
  388.8 2.1 copy.178
  390.9 1.3 collective-permute-start.1
  392.2 2.1 fusion.140
  395.2 1.7 collective-permute-done.1
  398.2 5.7 %scatter-add.6 = bf16[128,1792]{0,1:T(8,128)(2,1)} dynamic-update-slice(bf16[128,1792]{0,1:T(8,128)(2,1)} %split.8, bf16[3,1792]{0,1:T(8,128)(2,1)S(1)} %slice_add_fusion, s32[]{:T(128)} %constant.281.clone.1, s32[]{:T(128)} %constant.276.clone.1) | dynamic-update-slice | bytes 21508 | tf_op jit(solution)/shard_map/scatter-add | solution.py:242
  403.9 5.1 convolution_convert_fusion
  411.0 1.9 fusion.21
  413.0 1.6 convert_element_type.92
  414.6 96.7 %reduce-scatter.7.cloned.1.call-done = bf16[96,3352]{1,0:T(8,128)(2,1)} async-done(((bf16[768,3352]{1,0:T(8,128)(2,1)}), bf16[96,3352]{1,0:T(8,128)(2,1)}) %reduce-scatter.7.cloned.1.call-update) | async-done | bytes 643600 | tf_op jit(solution)/shard_map/reduce_scatter | solution.py:248
  511.5 4.6 fusion.59
  516.1 41.7 %all-reduce.14 = (f32[768]{0:T(1024)}, f32[1792,4]{0,1:T(4,128)}, f32[1792]{0:T(1024)}, f32[24]{0:T(128)}, f32[24]{0:T(128)}, /*index=5*/f32[24]{0:T(128)}, f32[1536]{0:T(1024)}) all-reduce(f32[768]{0:T(1024)S(1)} %get-tuple-element.338, f32[1792,4]{0,1:T(4,128)S(1)} %pad_add_fusion.1, ...), channel_id=1, replica_groups=mesh['dp'=4,'seq'=8] {'dp','seq'}, use_global_device_ids=true, to_apply=%region_26.28 | all-reduce | flops 11336 | bytes 90688 | tf_op jit(solution)/shard_map/psum | solution.py:270
  558.7 1.7 convert_element_type.90
  (235 shorter events, 36.7 us)
Async XLA Ops:
  7.2 72.0 %all-gather.8.cloned.1.call-start = ((), (), s32[]{:S(2)}) async-start(), calls=%async_computation.4 | async-start | bytes 5474304 | tf_op jit(solution)/shard_map/all_gather | solution.py:194
  7.9 153.6 %all-gather.12.cloned.1.call-start = ((), (), s32[]{:S(2)}) async-start(), calls=%async_computation.9 | async-start | bytes 3538944 | tf_op jit(solution)/shard_map/all_gather | solution.py:29
  8.9 82.8 %copy-start.30 = (f32[1792]{0:T(1024)}, f32[1792]{0:T(1024)S(1)}, u32[]{:S(2)}) copy-start(f32[1792]{0:T(1024)S(1)} %get-tuple-element.340) | copy-start | bytes 21508
  8.9 82.8 %copy-start.32 = (f32[1792]{0:T(1024)}, f32[1792]{0:T(1024)S(1)}, u32[]{:S(2)}) copy-start(f32[1792]{0:T(1024)S(1)} %get-tuple-element.341) | copy-start | bytes 21508
  9.0 82.8 %copy-start.34 = (f32[1792]{0:T(1024)}, f32[1792]{0:T(1024)S(1)}, u32[]{:S(2)}) copy-start(f32[1792]{0:T(1024)S(1)} %get-tuple-element.342) | copy-start | bytes 21508
  9.0 82.8 %copy-start.36 = (f32[1792]{0:T(1024)}, f32[1792]{0:T(1024)S(1)}, u32[]{:S(2)}) copy-start(f32[1792]{0:T(1024)S(1)} %get-tuple-element.343) | copy-start | bytes 21508
  10.0 73.9 %copy-start.64 = (f32[128]{0:T(128)}, f32[128]{0:T(128)S(1)}, u32[]{:S(2)}) copy-start(f32[128]{0:T(128)S(1)} %fusion.61) | copy-start | bytes 1540
  10.7 73.5 %copy-start.61 = (f32[24]{0:T(128)}, f32[24]{0:T(128)S(1)}, u32[]{:S(2)}) copy-start(f32[24]{0:T(128)S(1)} %exponential_negate_fusion) | copy-start | bytes 292
  12.3 71.6 %copy-start.19 = (bf16[128,768]{1,0:T(8,128)(2,1)}, bf16[128,768]{1,0:T(8,128)(2,1)S(1)}, u32[]{:S(2)}) copy-start(bf16[128,768]{1,0:T(8,128)(2,1)S(1)} %fusion.58) | copy-start | bytes 589828
  83.9 140.1 %copy-start = (f32[128,3352]{0,1:T(8,128)}, f32[128,3352]{0,1:T(8,128)S(1)}, u32[]{:S(2)}) copy-start(f32[128,3352]{0,1:T(8,128)S(1)} %fusion.145) | copy-start | bytes 5148676
  84.7 285.5 %copy-start.23 = (f32[128,24]{0,1:T(8,128)}, f32[128,24]{0,1:T(8,128)S(1)}, u32[]{:S(2)}) copy-start(f32[128,24]{0,1:T(8,128)S(1)} %get-tuple-element.381) | copy-start | bytes 36868
  85.3 6.5 %copy-start.53 = (f32[1792]{0:T(1024)S(1)}, f32[1792]{0:T(1024)}, u32[]{:S(2)}) copy-start(f32[1792]{0:T(1024)} %param.25) | copy-start | bytes 21508
  85.6 4.9 collective-permute-start
  98.5 63.3 %copy-start.4 = (f32[128,1792]{0,1:T(8,128)}, f32[128,1792]{0,1:T(8,128)S(1)}, u32[]{:S(2)}) copy-start(f32[128,1792]{0,1:T(8,128)S(1)} %get-tuple-element.378) | copy-start | bytes 2752516
  101.0 119.3 %all-gather.10.cloned.1.call-start = ((), (), s32[]{:S(2)}) async-start(), calls=%async_computation.5 | async-start | bytes 2433024 | tf_op jit(solution)/shard_map/all_gather | solution.py:221
  101.7 190.2 %reduce-scatter.9.cloned.1.call-start = ((), (), s32[]{:S(2)}) async-start(), calls=%async_computation.7 | async-start | bytes 2654208 | tf_op jit(solution)/shard_map/reduce_scatter | solution.py:255
  127.3 35.3 %copy-start.24 = (f32[128,128]{1,0:T(8,128)}, f32[128,128]{1,0:T(8,128)S(1)}, u32[]{:S(2)}) copy-start(f32[128,128]{1,0:T(8,128)S(1)} %fusion.96) | copy-start | bytes 196612
  163.1 4.6 copy-start.12
  167.7 52.6 %copy-start.2 = (f32[128,1536]{0,1:T(8,128)}, f32[128,1536]{0,1:T(8,128)S(1)}, u32[]{:S(2)}) copy-start(f32[128,1536]{0,1:T(8,128)S(1)} %get-tuple-element.377) | copy-start | bytes 2359300
  171.1 49.2 %copy-start.17 = (bf16[128,768]{1,0:T(8,128)(2,1)S(1)}, bf16[128,768]{1,0:T(8,128)(2,1)}, u32[]{:S(2)}) copy-start(bf16[128,768]{1,0:T(8,128)(2,1)} %param.31) | copy-start | bytes 589828
  171.1 182.2 %all-gather.14.cloned.1.call-start = ((), (), s32[]{:S(2)}) async-start(), calls=%async_computation.10 | async-start | bytes 3538944 | tf_op jit(solution)/shard_map/all_gather | solution.py:51
  229.0 184.0 %reduce-scatter.11.cloned.1.call-start = ((), (), s32[]{:S(2)}) async-start(), calls=%async_computation.8 | async-start | bytes 368640 | tf_op jit(solution)/shard_map/reduce_scatter | solution.py:263
  229.4 4.8 copy-start.9
  229.4 4.8 copy-start.25
  229.5 4.8 copy-start.28
  229.5 4.8 copy-start.38
  292.0 219.3 %reduce-scatter.7.cloned.1.call-start = ((), (), s32[]{:S(2)}) async-start(), calls=%async_computation.6 | async-start | bytes 5971968 | tf_op jit(solution)/shard_map/reduce_scatter | solution.py:248
  372.7 6.0 %copy-start.1 = (f32[128,3352]{0,1:T(8,128)S(1)}, f32[128,3352]{0,1:T(8,128)}, u32[]{:S(2)}) copy-start(f32[128,3352]{0,1:T(8,128)} %copy-done) | copy-start | bytes 5148676
  378.7 6.3 %copy-start.31 = (f32[1792]{0:T(1024)S(1)}, f32[1792]{0:T(1024)}, u32[]{:S(2)}) copy-start(f32[1792]{0:T(1024)} %copy-done.30) | copy-start | bytes 21508
  378.7 6.3 %copy-start.33 = (f32[1792]{0:T(1024)S(1)}, f32[1792]{0:T(1024)}, u32[]{:S(2)}) copy-start(f32[1792]{0:T(1024)} %copy-done.32) | copy-start | bytes 21508
  378.7 6.3 %copy-start.35 = (f32[1792]{0:T(1024)S(1)}, f32[1792]{0:T(1024)}, u32[]{:S(2)}) copy-start(f32[1792]{0:T(1024)} %copy-done.34) | copy-start | bytes 21508
  378.7 6.3 %copy-start.37 = (f32[1792]{0:T(1024)S(1)}, f32[1792]{0:T(1024)}, u32[]{:S(2)}) copy-start(f32[1792]{0:T(1024)} %copy-done.36) | copy-start | bytes 21508
  387.8 4.4 copy-start.58
  390.9 6.1 %collective-permute-start.1 = (f32[3,1792]{1,0:T(4,128)}, f32[3,1792]{1,0:T(4,128)}, u32[]{:S(2)}, u32[]{:S(2)}) collective-permute-start(f32[3,1792]{1,0:T(4,128)} %copy.178), channel_id=1, source_target_pairs={{1,0},{2,1},{3,2},{4,3},{5,4},{6,5},{7,6},{9,8},{10,9},{11,10},{12... | collective-permute-start | bytes 64520 | tf_op jit(solution)/shard_map/ppermute | solution.py:23
  398.0 5.9 %copy-start.21 = (bf16[768,128]{1,0:T(8,128)(2,1)S(1)}, bf16[768,128]{1,0:T(8,128)(2,1)}, u32[]{:S(2)}) copy-start(bf16[768,128]{1,0:T(8,128)(2,1)} %gather_fusion) | copy-start | bytes 589828
  398.1 5.9 %copy-start.49 = (pred[768]{0:T(1024)(128)(4,1)S(1)}, pred[768]{0:T(1024)(128)(4,1)}, u32[]{:S(2)}) copy-start(pred[768]{0:T(1024)(128)(4,1)} %compare_and_fusion) | copy-start | bytes 2308
  398.1 5.9 %copy-start.50 = (bf16[128,24]{0,1:T(8,128)(2,1)S(1)}, bf16[128,24]{0,1:T(8,128)(2,1)}, u32[]{:S(2)}) copy-start(bf16[128,24]{0,1:T(8,128)(2,1)} %get-tuple-element.374) | copy-start | bytes 18436
  409.1 149.6 %reduce-scatter.13.cloned.1.call-start = ((), (), s32[]{:S(2)}) async-start(), calls=%async_computation.11 | async-start | bytes 829440
  411.0 100.4 %copy-start.66 = (f32[24]{0:T(128)S(1)}, f32[24]{0:T(128)}, u32[]{:S(2)}) copy-start(f32[24]{0:T(128)} %get-tuple-element.388) | copy-start | bytes 292
  411.0 100.4 %copy-start.70 = (f32[24]{0:T(128)S(1)}, f32[24]{0:T(128)}, u32[]{:S(2)}) copy-start(f32[24]{0:T(128)} %param.27) | copy-start | bytes 292
  411.0 100.4 %copy-start.51 = (bf16[128,24]{0,1:T(8,128)(2,1)S(1)}, bf16[128,24]{0,1:T(8,128)(2,1)}, u32[]{:S(2)}) copy-start(bf16[128,24]{0,1:T(8,128)(2,1)} %get-tuple-element.374) | copy-start | bytes 18436
  411.0 100.4 %copy-start.52 = (f32[768]{0:T(1024)S(1)}, f32[768]{0:T(1024)}, u32[]{:S(2)}) copy-start(f32[768]{0:T(1024)} %param.22) | copy-start | bytes 9220
  411.0 100.4 %copy-start.60 = (f32[128]{0:T(128)S(1)}, f32[128]{0:T(128)}, u32[]{:S(2)}) copy-start(f32[128]{0:T(128)} %copy-done.59) | copy-start | bytes 1540
  511.4 4.6 copy-start.41
  511.5 4.6 copy-start.42
  511.5 4.6 copy-start.62
  511.5 46.3 %copy-start.65 = (f32[128]{0:T(128)S(1)}, f32[128]{0:T(128)}, u32[]{:S(2)}) copy-start(f32[128]{0:T(128)} %copy-done.64) | copy-start | bytes 1540
  511.5 46.3 %copy-start.18 = (bf16[128,768]{1,0:T(8,128)(2,1)S(1)}, bf16[128,768]{1,0:T(8,128)(2,1)}, u32[]{:S(2)}) copy-start(bf16[128,768]{1,0:T(8,128)(2,1)} %param.31) | copy-start | bytes 589828
  (33 other events, 68.1 us)
Sparse Core Ops, SparseCore 0:
  10.8 68.3 all-gather.7
  101.1 60.3 all-gather.11
  164.5 55.7 all-gather.9
  223.6 68.3 reduce-scatter.8
  294.0 59.2 all-gather.13
  355.6 18.9 reduce-scatter.10
  409.2 102.0 reduce-scatter.6
  513.9 21.9 reduce-scatter.12
where the time goes:
time: 575 us; the launch traced here: 568 us
  waiting for transfers between devices  359 us (62%)
  blocking collectives  61.9 us (11%)
  other arithmetic  49.7 us (9%)
  matrix products  46.3 us (8%)
  local copies, waits for them, and re-layouts  29 us (5%)
  between operations  15.6 us (3%)
    reduce_scatter x1, waiting for transfers between devices, body(): lax.psum_scatter(contract_rows(jnp.take(normed, picked, axis=1), projecte...  96.7 us
    all_gather x1, waiting for transfers between devices, body(): lax.all_gather(in_proj, ('dp', 'seq'), axis=0, tiled=True)  66.9 us
    all_gather x1, waiting for transfers between devices, prefix_2(): lax.all_gather(a.astype(kind), axis)  61.2 us
    all_gather x1, waiting for transfers between devices, body(): lax.all_gather(out_proj, ('dp', 'seq'), axis=0, tiled=True)  49.1 us
    reduce_scatter x1, waiting for transfers between devices, body(): lax.psum_scatter(contract_rows(jnp.take(cotangent, picked, axis=1), gated...  49.1 us
    psum x1, blocking collectives, body(): lax.psum((norm_gain_grad, conv_weight_grad, conv_bias_grad, dt_bias_grad,...  41.7 us
    all_gather x1, waiting for transfers between devices, prefix(): lax.all_gather(a.astype(kind), axis)  32.5 us
    all_gather x1, blocking collectives, prefix(): lax.all_gather(a.astype(kind), axis)  20.2 us
  transfers between devices with their start and end apart: 10, of which 8 were waited for; matrix products, arithmetic and copies ran while one was open for 18% of the time, Pallas kernels for 0%

commit v1 on v0

v1 whole, which is shorter than its diff:
```python
from functools import partial

import jax
import jax.numpy as jnp
from jax import lax
from jax.experimental import pallas as pl
from jax.experimental.pallas import tpu as pltpu
from jax.sharding import PartitionSpec as P

HEADS = 24
HEAD_DIM = 64
STATE = 128
CONV = 4
DI = 1536
XBC = 1792
PROJ = DI + XBC + HEADS
LANES = 128
WIDE = -(-PROJ // LANES) * LANES


EPS = 1e-05
HIGH = lax.Precision.HIGHEST
MESH = pl.DeviceIdType.MESH
VMEM_BYTES = 60 * 1024 * 1024


def bits_of(count):
    return count.bit_length() - 1


def bit_at(place, bit):
    return (place // 2**bit) % 2


def places():
    return lax.axis_index("dp"), lax.axis_index("seq")


def partner(bit, seq_bits):
    dp_at, seq_at = places()
    if bit < seq_bits:
        return dp_at, seq_at + (1 - 2 * bit_at(seq_at, bit)) * 2**bit
    up = bit - seq_bits
    return dp_at + (1 - 2 * bit_at(dp_at, up)) * 2**up, seq_at


def greet(bits, seq_bits):
    barrier = pltpu.get_barrier_semaphore()
    for bit in range(bits):
        pl.semaphore_signal(barrier, inc=1, device_id=partner(bit, seq_bits), device_id_type=MESH)
    pl.semaphore_wait(barrier, bits)


def gather_orders(seq_bits, dp_bits):
    x_count = seq_bits // 2
    x_bits = list(range(x_count))
    z_bits = list(range(x_count, seq_bits))[::-1]
    core = [seq_bits]
    y_bits = [seq_bits + 1 + i for i in range(dp_bits - 1)]
    return (
        z_bits + x_bits + y_bits + core,
        z_bits + y_bits + x_bits + core,
        x_bits + z_bits[:1] + y_bits + z_bits[1:] + core,
        y_bits + z_bits[:1] + x_bits + z_bits[1:] + core,
    )


def split_lanes(width, count):
    tiles = width // LANES
    edges = [tiles * i // count * LANES for i in range(count + 1)]
    return [(low, high - low) for low, high in zip(edges, edges[1:])]


def gather_kernel(seq_bits, streams, bits, *refs):
    array_count = 1 + max(stream[0] for stream in streams)
    shards, outs = refs[:array_count], refs[array_count : 2 * array_count]
    send_sem, recv_sem, own_sem = refs[2 * array_count :]
    dp_at, seq_at = places()
    place = dp_at * 2**seq_bits + seq_at
    own = [
        pltpu.make_async_copy(shard, out.at[place], own_sem.at[i])
        for i, (shard, out) in enumerate(zip(shards, outs))
    ]
    for copy in own:
        copy.start()
    greet(bits, seq_bits)
    for copy in own:
        copy.wait()

    def landed(stream, stage, sem):
        which, low, width, _ = streams[stream]
        view = outs[which].at[pl.ds(0, 2**stage), :, pl.ds(low, width)]
        pltpu.make_async_copy(view, view, sem.at[stream, stage]).wait()

    for stage in range(bits + 1):
        for stream, (which, low, width, order) in enumerate(streams):
            if stage > 0:
                landed(stream, stage - 1, recv_sem)
            if stage == bits:
                continue
            free = order[:stage]
            run = 0
            while run in free:
                run += 1
            base = place
            for bit in free:
                base = base - bit_at(place, bit) * 2**bit
            upper = [bit for bit in free if bit > run]
            for combo in range(2 ** len(upper)):
                start = base + sum(2**bit for i, bit in enumerate(upper) if combo >> i & 1)
                view = outs[which].at[pl.ds(start, 2**run), :, pl.ds(low, width)]
                pltpu.make_async_remote_copy(
                    src_ref=view,
                    dst_ref=view,
                    send_sem=send_sem.at[stream, stage],
                    recv_sem=recv_sem.at[stream, stage],
                    device_id=partner(order[stage], seq_bits),
                    device_id_type=MESH,
                ).start()
    for stage in range(bits):
        for stream in range(len(streams)):
            landed(stream, stage, send_sem)


def gather_all(shards, collective_id):
    seq_bits, dp_bits = bits_of(lax.axis_size("seq")), bits_of(lax.axis_size("dp"))
    bits = seq_bits + dp_bits
    orders = gather_orders(seq_bits, dp_bits)
    streams = [
        (which, low, width, order)
        for which, shard in enumerate(shards)
        for (low, width), order in zip(split_lanes(shard.shape[1], len(orders)), orders)
    ]
    return pl.pallas_call(
        partial(gather_kernel, seq_bits, streams, bits),
        out_shape=[jax.ShapeDtypeStruct((2**bits, *a.shape), a.dtype) for a in shards],
        in_specs=[pl.BlockSpec(memory_space=pltpu.VMEM)] * len(shards),
        out_specs=[pl.BlockSpec(memory_space=pl.ANY)] * len(shards),
        scratch_shapes=[
            pltpu.SemaphoreType.DMA((len(streams), bits)),
            pltpu.SemaphoreType.DMA((len(streams), bits)),
            pltpu.SemaphoreType.DMA((len(shards),)),
        ],
        compiler_params=pltpu.CompilerParams(
            collective_id=collective_id, has_side_effects=True, vmem_limit_bytes=VMEM_BYTES
        ),
        name="gather_rows",
    )(*shards)


def sum_kernel(seq_bits, streams, bits, array_count, *refs):
    terms, vector = refs[:array_count], refs[array_count]
    outs, vector_out = refs[array_count + 1 : 2 * array_count + 1], refs[2 * array_count + 1]
    held = refs[2 * array_count + 2 : 2 * array_count + 2 + len(streams) * bits]
    rest = refs[2 * array_count + 2 + len(streams) * bits :]
    vector_in, vector_sum, send_sem, recv_sem, vector_send, vector_recv = rest
    dp_at, seq_at = places()
    place = dp_at * 2**seq_bits + seq_at
    greet(bits, seq_bits)

    def source(stream, stage):
        which, low, width, _ = streams[stream]
        if stage == 0:
            return terms[which], pl.ds(low, width)
        return held[stream * bits + stage - 1], pl.ds(0, width)

    def position(stream, stage):
        order = streams[stream][3]
        remaining = sorted(order[stage:])
        return remaining.index(order[stage]), bit_at(place, order[stage])

    def landed(stream, stage, sem):
        view = held[stream * bits + stage]
        pltpu.make_async_copy(view, view, sem.at[stream, stage]).wait()

    def vector_copy(stage):
        return pltpu.make_async_remote_copy(
            src_ref=vector if stage == 0 else vector_sum.at[stage - 1],
            dst_ref=vector_in.at[stage],
            send_sem=vector_send.at[stage],
            recv_sem=vector_recv.at[stage],
            device_id=partner(stage, seq_bits),
            device_id_type=MESH,
        )

    for stage in range(bits + 1):
        if stage > 0:
            vector_copy(stage - 1).wait_recv()
            before = vector[...] if stage == 1 else vector_sum[stage - 2]
            total = before + vector_in[stage - 1]
            if stage < bits:
                vector_sum[stage - 1] = total
            else:
                vector_out[...] = total
        if stage < bits:
            vector_copy(stage).start()
        for stream, (which, low, width, order) in enumerate(streams):
            if stage > 0:
                landed(stream, stage - 1, recv_sem)
                spot, mine = position(stream, stage - 1)
                kept, lanes = source(stream, stage - 1)
                came = held[stream * bits + stage - 1]
                if stage == bits:
                    outs[which][:, pl.ds(low, width)] = kept[mine, :, lanes].astype(
                        jnp.float32
                    ) + came[0].astype(jnp.float32)
                    continue

                def add_one(block, carry, spot=spot, mine=mine, kept=kept, lanes=lanes, came=came):
                    from_block = (block // 2**spot) * 2 ** (spot + 1) + mine * 2**spot
                    from_block = from_block + block % 2**spot
                    added = kept[from_block, :, lanes].astype(jnp.float32) + came[block].astype(
                        jnp.float32
                    )
                    came[block] = added.astype(came.dtype)
                    return carry

                lax.fori_loop(0, 2 ** (bits - stage), add_one, 0)
            spot, mine = position(stream, stage)
            sent, lanes = source(stream, stage)
            for high in range(2 ** (bits - stage - 1 - spot)):
                start = high * 2 ** (spot + 1) + (1 - mine) * 2**spot
                pltpu.make_async_remote_copy(
                    src_ref=sent.at[pl.ds(start, 2**spot), :, lanes],
                    dst_ref=held[stream * bits + stage].at[pl.ds(high * 2**spot, 2**spot)],
                    send_sem=send_sem.at[stream, stage],
                    recv_sem=recv_sem.at[stream, stage],
                    device_id=partner(order[stage], seq_bits),
                    device_id_type=MESH,
                ).start()
    for stage in range(bits):
        vector_copy(stage).wait_send()
        for stream in range(len(streams)):
            landed(stream, stage, send_sem)


def sum_to_owners(terms, vector, collective_id):
    seq_bits, dp_bits = bits_of(lax.axis_size("seq")), bits_of(lax.axis_size("dp"))
    bits = seq_bits + dp_bits
    orders = [order[::-1] for order in gather_orders(seq_bits, dp_bits)]
    terms = [term.reshape(2**bits, -1, term.shape[1]) for term in terms]
    streams = [
        (which, low, width, order)
        for which, term in enumerate(terms)
        for (low, width), order in zip(split_lanes(term.shape[2], len(orders)), orders)
    ]
    rows = terms[0].shape[1]
    in_vmem = pl.BlockSpec(memory_space=pltpu.VMEM)
    held = [
        pltpu.VMEM((2 ** (bits - 1 - stage), rows, width), jnp.bfloat16)
        for _, _, width, _ in streams
        for stage in range(bits)
    ]
    return pl.pallas_call(
        partial(sum_kernel, seq_bits, streams, bits, len(terms)),
        out_shape=[jax.ShapeDtypeStruct(a.shape[1:], jnp.float32) for a in terms]
        + [jax.ShapeDtypeStruct(vector.shape, vector.dtype)],
        in_specs=[in_vmem] * (len(terms) + 1),
        out_specs=[in_vmem] * (len(terms) + 1),
        scratch_shapes=held
        + [
            pltpu.VMEM((bits, *vector.shape), jnp.float32),
            pltpu.VMEM((bits, *vector.shape), jnp.float32),
            pltpu.SemaphoreType.DMA((len(streams), bits)),
            pltpu.SemaphoreType.DMA((len(streams), bits)),
            pltpu.SemaphoreType.DMA((bits,)),
            pltpu.SemaphoreType.DMA((bits,)),
        ],
        compiler_params=pltpu.CompilerParams(
            collective_id=collective_id, has_side_effects=True, vmem_limit_bytes=VMEM_BYTES
        ),
        name="sum_rows",
    )(*terms, vector)


def scan_kernel(count, reverse, state, decay, out, came, came_decay, ready, *sems):
    out_send, out_recv, decay_send, decay_recv, back_send, back_recv = sems
    dp_at, seq_at = places()
    barrier = pltpu.get_barrier_semaphore()
    peers = [(seq_at + hop) % count for hop in range(1, count)]
    for peer in peers:
        pl.semaphore_signal(barrier, inc=1, device_id=(dp_at, peer), device_id_type=MESH)
    pl.semaphore_wait(barrier, count - 1)

    def copy(hop, which):
        target = (seq_at + hop) % count
        source, landing, send_sem, recv_sem = (
            (state.at[target], came.at[seq_at], out_send, out_recv),
            (decay, came_decay.at[seq_at], decay_send, decay_recv),
            (ready.at[target], out.at[seq_at], back_send, back_recv),
        )[which]
        return pltpu.make_async_remote_copy(
            src_ref=source,
            dst_ref=landing,
            send_sem=send_sem.at[hop],
            recv_sem=recv_sem.at[hop],
            device_id=(dp_at, target),
            device_id_type=MESH,
        )

    for hop in range(1, count):
        copy(hop, 0).start()
        copy(hop, 1).start()
    came[seq_at] = state[seq_at]
    came_decay[seq_at] = decay[...]
    for hop in range(1, count):
        copy(hop, 0).wait_recv()
        copy(hop, 1).wait_recv()
    total = jnp.zeros(state.shape[1:], jnp.float32)
    for place in range(count)[:: -1 if reverse else 1]:
        ready[place] = total.astype(ready.dtype)
        total = came_decay[place] * total + came[place].astype(jnp.float32)
    for hop in range(1, count):
        copy(hop, 2).start()
    out[seq_at] = ready[seq_at]
    for hop in range(1, count):
        copy(hop, 2).wait_recv()
    for hop in range(1, count):
        for which in range(3):
            copy(hop, which).wait_send()


def scan_states(state, decay, reverse, collective_id):
    count = lax.axis_size("seq")
    state = state.astype(jnp.bfloat16).reshape(count, STATE // count, DI)
    in_vmem = pl.BlockSpec(memory_space=pltpu.VMEM)
    sems = [pltpu.SemaphoreType.DMA((count,))] * 6
    got = pl.pallas_call(
        partial(scan_kernel, count, reverse),
        out_shape=jax.ShapeDtypeStruct(state.shape, state.dtype),
        in_specs=[in_vmem, in_vmem],
        out_specs=in_vmem,
        scratch_shapes=[
            pltpu.VMEM(state.shape, state.dtype),
            pltpu.VMEM((count, 1, DI), jnp.float32),
            pltpu.VMEM(state.shape, state.dtype),
        ]
        + sems,
        compiler_params=pltpu.CompilerParams(
            collective_id=collective_id, has_side_effects=True, vmem_limit_bytes=VMEM_BYTES
        ),
        name="scan_back" if reverse else "scan_states",
    )(state, decay[None, :])
    return got.reshape(STATE, DI).astype(jnp.float32)


def passed_along(value, axis, steps):
    count = lax.axis_size(axis)
    first, last = (max(0, -steps), min(count, count - steps))
    return lax.ppermute(value, axis, [(source, source + steps) for source in range(first, last)])


def pre_norm(residual_in, norm_gain):
    scale_rms = lax.rsqrt(jnp.mean(residual_in * residual_in, axis=-1, keepdims=True) + EPS)
    return residual_in * scale_rms * norm_gain


def conv_silu(padded, conv_weight, conv_bias, row_count):
    total = jnp.zeros((row_count, padded.shape[1]), jnp.float32) + conv_bias[None, :]
    for offset in range(conv_weight.shape[1]):
        total = total + conv_weight[:, offset][None, :] * padded[offset : offset + row_count]
    return jax.nn.silu(total)


def spread_heads(by_head):
    return jnp.repeat(by_head, HEAD_DIM, axis=-1)


def ssd_block(xs, b_block, c_block, step_block, decay_block):
    row_count = xs.shape[0]
    at = jnp.arange(row_count)
    lower = at[:, None] >= at[None, :]
    cumulative = jnp.dot(lower.astype(jnp.float32), decay_block, precision=HIGH)
    by_head = cumulative.T
    spread = by_head[:, :, None] - by_head[:, None, :]
    weights_mat = jnp.exp(jnp.where(lower[None], spread, -jnp.inf))
    intersection = jnp.dot(c_block, b_block.T, precision=HIGH)
    scaled_x = xs * spread_heads(step_block)
    scores = weights_mat * intersection[None]
    output = jnp.einsum(
        "hts,shp->thp", scores, scaled_x.reshape(row_count, HEADS, HEAD_DIM), precision=HIGH
    )
    tail = jnp.exp(cumulative[-1][None, :] - cumulative)
    fresh = jnp.dot(b_block.T, scaled_x * spread_heads(tail), precision=HIGH)
    return output.reshape(row_count, DI), cumulative, fresh


def mid_local(xbc, dt_raw, edge, conv_weight, conv_bias, dt_bias, a_log):
    row_count = xbc.shape[0]
    activated = conv_silu(jnp.concatenate([edge, xbc], axis=0), conv_weight, conv_bias, row_count)
    xs = activated[:, :DI]
    b_mat = activated[:, DI : DI + STATE]
    c_mat = activated[:, DI + STATE :]
    step = jax.nn.softplus(dt_raw + dt_bias)
    log_decay = step * -jnp.exp(a_log)
    ssd_out, cumulative, final = ssd_block(xs, b_mat, c_mat, step, log_decay)
    return (ssd_out, xs, c_mat, cumulative, final)


def post_gate(ssd_out, xs, gate_part, skip_gain, gated_gain):
    row_count = xs.shape[0]
    skipped = (xs.reshape(row_count, HEADS, HEAD_DIM) * skip_gain[None, :, None]).reshape(
        row_count, DI
    )
    mixed_in = (ssd_out + skipped) * jax.nn.silu(gate_part)
    scale_rms = lax.rsqrt(jnp.mean(mixed_in * mixed_in, axis=-1, keepdims=True) + EPS)
    return mixed_in * scale_rms * gated_gain


def contract_rows(left, right):
    return lax.dot_general(
        left, right, (((0,), (0,)), ((), ())), preferred_element_type=jnp.float32
    )


def contract_cols(left, right):
    return lax.dot_general(
        left, right, (((1,), (1,)), ((), ())), preferred_element_type=jnp.float32
    )


def body(
    inputs,
    norm_gain,
    in_proj,
    conv_weight,
    conv_bias,
    dt_bias,
    a_log,
    skip_gain,
    gated_gain,
    out_proj,
    cotangent,
):
    row_count = inputs.shape[0]
    residual_in = inputs.astype(jnp.float32)
    normed_full, norm_back = jax.vjp(pre_norm, residual_in, norm_gain)
    normed = normed_full.astype(jnp.bfloat16)
    in_whole, out_whole = gather_all(
        [jnp.pad(in_proj, ((0, 0), (0, WIDE - PROJ))), out_proj], collective_id=1
    )
    in_whole = in_whole.reshape(-1, WIDE)
    out_whole = out_whole.reshape(-1, DI)
    projected = jnp.dot(normed, in_whole, preferred_element_type=jnp.float32)
    gate_part = projected[:, :DI]
    xbc = projected[:, DI : DI + XBC]
    dt_raw = projected[:, DI + XBC : PROJ]
    edge = passed_along(xbc[row_count - (CONV - 1) :], "seq", 1)
    primal, mid_back = jax.vjp(
        mid_local, xbc, dt_raw, edge, conv_weight, conv_bias, dt_bias, a_log
    )
    local_out, xs, c_mat, cumulative, s_local = primal
    decay = jnp.exp(cumulative[-1])
    wide_decay = spread_heads(decay)
    state_in = scan_states(s_local, wide_decay, False, collective_id=2)
    weighted = spread_heads(jnp.exp(cumulative))
    carried_part = jnp.dot(c_mat, state_in, precision=HIGH) * weighted
    ssd_out = local_out + carried_part
    gated_full, post_back = jax.vjp(post_gate, ssd_out, xs, gate_part, skip_gain, gated_gain)
    gated = gated_full.astype(jnp.bfloat16)
    mixed = contract_cols(gated, out_whole)
    layer_out = (residual_in + mixed).astype(jnp.bfloat16)
    gated_cot = jnp.dot(cotangent, out_whole, preferred_element_type=jnp.float32)
    ssd_cot, xs_cot, gate_cot, skip_grad, gated_gain_grad = post_back(gated_cot)
    scaled_cot = ssd_cot * weighted
    local_grad = jnp.dot(c_mat.T, scaled_cot, precision=HIGH)
    later_grad = scan_states(local_grad, wide_decay, True, collective_id=3)
    c_cot = lax.dot_general(scaled_cot, state_in, (((1,), (1,)), ((), ())), precision=HIGH)
    cum_cot = jnp.sum((ssd_cot * carried_part).reshape(row_count, HEADS, HEAD_DIM), axis=2)
    last_cot = jnp.sum(later_grad * state_in, axis=0).reshape(HEADS, HEAD_DIM).sum(axis=1) * decay
    is_last = (jnp.arange(row_count) == row_count - 1)[:, None]
    cum_cot = cum_cot + jnp.where(is_last, last_cot[None, :], 0.0)
    mid_grads = mid_back((ssd_cot, xs_cot, c_cot, cum_cot, later_grad))
    xbc_cot, dt_cot, edge_cot, conv_weight_grad, conv_bias_grad, dt_bias_grad, a_log_grad = (
        mid_grads
    )
    edge_back = passed_along(edge_cot, "seq", -1)
    xbc_cot = xbc_cot + jnp.pad(edge_back, ((row_count - (CONV - 1), 0), (0, 0)))
    projected_cot = jnp.concatenate(
        [gate_cot, xbc_cot, dt_cot, jnp.zeros((row_count, WIDE - PROJ), jnp.float32)], axis=1
    ).astype(jnp.bfloat16)
    in_term = contract_rows(normed, projected_cot).astype(jnp.bfloat16)
    out_term = contract_rows(cotangent, gated).astype(jnp.bfloat16)
    normed_cot = contract_cols(projected_cot, in_whole)
    input_part, norm_gain_grad = norm_back(normed_cot)
    input_grad = cotangent.astype(jnp.float32) + input_part
    small = (
        norm_gain_grad,
        conv_weight_grad.T,
        conv_bias_grad,
        gated_gain_grad,
        dt_bias_grad,
        a_log_grad,
        skip_grad,
    )
    flat = jnp.concatenate([a.reshape(-1) for a in small])
    tile = 8 * LANES
    flat = jnp.pad(flat, (0, -flat.shape[0] % tile))
    in_proj_grad, out_proj_grad, summed = sum_to_owners(
        [in_term, out_term], flat.reshape(-1, LANES), collective_id=4
    )
    summed = summed.reshape(-1)
    parts, at = [], 0
    for a in small:
        parts.append(summed[at : at + a.size].reshape(a.shape))
        at += a.size
    return (
        layer_out,
        input_grad,
        in_proj_grad[:, :PROJ],
        out_proj_grad,
        parts[0],
        parts[1].T,
        parts[2],
        parts[4],
        parts[5],
        parts[6],
        parts[3],
    )


def solution(mesh):
    placed = (
        P(("dp", "seq"), None),
        P(),
        P(("dp", "seq"), None),
        P(),
        P(),
        P(),
        P(),
        P(),
        P(),
        P(("dp", "seq"), None),
        P(("dp", "seq"), None),
    )
    return jax.shard_map(
        body,
        mesh=mesh,
        in_specs=placed,
        out_specs=(
            P(("dp", "seq"), None),
            P(("dp", "seq"), None),
            P(("dp", "seq"), None),
            P(("dp", "seq"), None),
            P(),
            P(),
            P(),
            P(),
            P(),
            P(),
            P(),
        ),
        check_vma=False,
    )
```

time: 575 us -> 259 us (0.45); the launches traced: 568 us -> 258 us
  waiting for transfers between devices: 359 us -> 0.01 us
  Pallas kernels: 0 us -> 157 us
  blocking collectives: 61.9 us -> 0 us
  other arithmetic: 49.7 us -> 17.3 us
  between operations: 15.6 us -> 1.52 us
    all_gather x4 -> x0, waiting for transfers between devices: 210 us -> none  [the longest x1 66.9 us: body(): lax.all_gather(in_proj, ('dp', 'seq'), axis=0, tiled=True)]
    pallas_call x0 -> x4, Pallas kernels: none -> 157 us  [the longest x1 56.4 us: sum_to_owners(): pl.pallas_call(partial(sum_kernel, seq_bits, streams, bits, len(terms)),...]
    reduce_scatter x3 -> x0, waiting for transfers between devices: 146 us -> none  [the longest x1 96.7 us: body(): lax.psum_scatter(contract_rows(jnp.take(normed, picked, axis=1), projecte...]
    psum x1 -> x0, blocking collectives: 41.7 us -> none  [body(): lax.psum((norm_gain_grad, conv_weight_grad, conv_bias_grad, dt_bias_grad,...]
    all_gather x1 -> x0, blocking collectives: 20.2 us -> none  [prefix(): lax.all_gather(a.astype(kind), axis)]
    convert_element_type x11 -> x0, other arithmetic: 9.29 us -> none  [the longest x7 4.84 us: one(): lax.dynamic_index_in_dim(a, source, 0, False).astype(own.dtype)]
    add x8 -> x0, other arithmetic: 8.51 us -> none  [the longest x7 8.39 us: reverse_chain(): later[1] + later[0][:, None, None] * earlier[1]]
    reshape x0 -> x9, local copies, waits for them, and re-layouts: none -> 8.51 us  [the longest x3 2.58 us: spread_heads(): return jnp.repeat(by_head, HEAD_DIM, axis=-1)]
  transfers between devices with their start and end apart: 10 -> 2, of which waited for: 8 -> 0; matrix products, arithmetic and copies ran while one was open for 18% -> 5% of each run, Pallas kernels for 0% -> 0%
where the time goes in v1:
time: 259 us; the launch traced here: 258 us
  Pallas kernels  157 us (61%)
  matrix products  47.1 us (18%)
  local copies, waits for them, and re-layouts  29.6 us (11%)
  other arithmetic  17.3 us (7%)
  starting transfers between devices  5.25 us (2%)
    pallas_call x1, Pallas kernels, sum_to_owners(): pl.pallas_call(partial(sum_kernel, seq_bits, streams, bits, len(terms)),...  56.4 us
    pallas_call x1, Pallas kernels, gather_all(): pl.pallas_call(partial(gather_kernel, seq_bits, streams, bits), out_shape...  50.7 us
    pallas_call x2, Pallas kernels, scan_states(): pl.pallas_call(partial(scan_kernel, count, reverse), out_shape=jax.ShapeD...  50 us
    dot_general x3, matrix products, ssd_block(): jnp.einsum('hts,shp->thp', scores, scaled_x.reshape(row_count, HEADS, HEA...  12.4 us
    dot_general x3, matrix products, ssd_block(): fresh = jnp.dot(b_block.T, scaled_x * spread_heads(tail), precision=HIGH)  7.7 us
    dot_general x2, matrix products, contract_rows(): lax.dot_general(left, right, (((0,), (0,)), ((), ())), preferred_element_...  6.28 us
    slice x5, local copies, waits for them, and re-layouts, body(): parts.append(summed[at:at + a.size].reshape(a.shape))  6.08 us
    dot_general x2, matrix products, contract_cols(): lax.dot_general(left, right, (((1,), (1,)), ((), ())), preferred_element_...  5.82 us
  transfers between devices with their start and end apart: 2, of which 0 were waited for; matrix products, arithmetic and copies ran while one was open for 5% of the time, Pallas kernels for 0%

profile of v1, /device:TPU:0, one launch (start us, length us, event | category | flops | bytes accessed | tf_op | source)
XLA Modules:
  0.0 257.8 jit_solution(17041201722766550203)
XLA Ops:
  0.6 1.0 fusion.33
  2.2 1.6 pad.48.refs_0_
  3.8 50.7 %gather_rows.1 = (bf16[32,24,3456]{2,1,0:T(8,128)(2,1)}, bf16[32,24,1536]{2,1,0:T(8,128)(2,1)}) custom-call(bf16[24,3456]{1,0:T(8,128)(2,1)} %pad.48.refs_0_, bf16[24,1536]{1,0:T(8,128)(2,1)} %refs_1_.1), custom_call_target="tpu_custom_call" | custom-call | tf_op jit(solution)/shard_map/gather_rows/pallas_call | solution.py:134
  54.6 3.6 %fusion.41 = f32[128,3456]{1,0:T(8,128)S(1)} fusion(bf16[768,3456]{1,0:T(8,128)(2,1)} %bitcast.70, bf16[128,768]{1,0:T(8,128)(2,1)} %param.11, f32[768]{0:T(1024)} %param.12, f32[128]{0:T(128)S(1)} %fusion.72), kind=kOutput, calls=%fused_computation.88 | convolution fusion | flops 679870464 | bytes 7278080 | tf_op jit(solution)/shard_map/dot_general | solution.py:444
  58.2 3.6 %collective-permute-start = (f32[3,1792]{1,0:T(4,128)S(1)}, f32[3,1792]{1,0:T(4,128)S(1)}, u32[]{:S(2)}, u32[]{:S(2)}) collective-permute-start(f32[3,1792]{1,0:T(4,128)S(1)} %slice.107), channel_id=1, source_target_pairs={{0,1},{1,2},{2,3},{3,4},{4,5},{5,6},{6,7},{8,9},{9,10},{10,11},{11... | collective-permute-start | bytes 64520 | tf_op jit(solution)/shard_map/ppermute | solution.py:350
  64.6 1.0 slice.108
  65.7 0.7 mul.363
  66.8 1.2 copy.100
  68.0 1.2 copy.103
  69.9 4.0 %fusion.13 = (f32[128,1792]{1,0:T(8,128)S(1)}, f32[128,1792]{1,0:T(8,128)}) fusion(f32[128,1792]{1,0:T(8,128)} %slice.108, f32[1792]{0:T(1024)S(1)} %get-tuple-element.35, f32[3,1792]{1,0:T(4,128)S(1)} %collective-permute-done, f32[1792]{0:T(1024)S(1)} %copy-done.33, f32[1792]{0:T(1024)S(1)} %get-tuple-element.34, f32[1792]{0:T(1024)S(1)} %get-tuple-element.33, ...), kind=kLoop, calls=%fused_computation.38 | loop fusion | flops 3440640 | bytes 2809856 | tf_op jit(solution)/shard_map/jvp(jit(silu))/mul | solution.py:362
  73.9 0.9 fusion.47
  74.8 2.5 fusion.82
  77.2 2.3 copy.101
  79.5 5.3 %fusion.3 = f32[24,64,128]{2,1,0:T(8,128)} fusion(f32[128,24,64]{0,2,1:T(8,128)} %bitcast.87, f32[128,128]{1,0:T(8,128)} %fusion.47, f32[24,128]{1,0:T(8,128)S(1)} %bitcast.94, pred[128,128]{1,0:T(8,128)(4,1)} %iota_compare_fusion), kind=kOutput, calls=%fused_computation.11 | convolution fusion | flops 303169536 | bytes 1667072 | tf_op jit(solution)/shard_map/jvp(hts,shp->thp)/dot_general | solution.py:380
  84.9 2.3 copy.104
  87.2 1.6 convolution_convert_fusion.3
  88.8 28.3 %scan_states.1 = bf16[8,16,1536]{2,1,0:T(8,128)(2,1)} custom-call(bf16[8,16,1536]{2,1,0:T(8,128)(2,1)} %bitcast.85, f32[1,1536]{1,0:T(1,128)} %broadcast_in_dim_reshape.4.decay), custom_call_target="tpu_custom_call" | custom-call | tf_op jit(solution)/shard_map/scan_states/pallas_call | solution.py:328
  117.2 3.2 %multiply_reduce_fusion.9 = (f32[128]{0:T(128)S(1)}, f32[128,1536]{1,0:T(8,128)S(1)}, f32[128,1536]{1,0:T(8,128)S(1)}, f32[128,1536]{1,0:T(8,128)}) fusion(f32[128,3456]{1,0:T(8,128)S(1)} %fusion.41, f32[1536]{0:T(1024)S(1)} %copy-done.41, f32[128,1792]{1,0:T(8,128)S(1)} %get-tuple-element.47, f32[128,1536]{1,0:T(8,128)} %copy.104, f32[128,1536]{1,0:T(8,128)} %copy.103, ...), kind=kOutput, calls=%fused_computation.50 | convolution fusion | flops 304152448 | bytes 5972480 | tf_op jit(solution)/shard_map/dot_general | solution.py:457
  120.4 1.6 fusion.5
  122.0 1.1 multiply_reduce_fusion.6
  123.2 1.9 multiply_reduce_fusion.5
  125.2 1.2 copy.106
  126.4 2.9 %convolution_convert_fusion.2 = bf16[128,1536]{1,0:T(8,128)(2,1)} fusion(f32[128,1536]{1,0:T(8,128)S(1)} %get-tuple-element.38, f32[128,1536]{1,0:T(8,128)} %copy.103, f32[128,1792]{1,0:T(8,128)} %copy-done), kind=kOutput, calls=%fused_computation.4 | convolution fusion | flops 302383104 | bytes 2031616 | tf_op jit(solution)/shard_map/dot_general | solution.py:466
  129.3 2.7 %fusion.1 = f32[24,64,128]{2,1,0:T(8,128)} fusion(f32[24,64,128]{2,1,0:T(8,128)S(1)} %bitcast.90, f32[128,128]{1,0:T(8,128)S(1)} %copy-done.35, f32[24,128]{1,0:T(8,128)S(1)} %bitcast.95, pred[128,128]{1,0:T(8,128)(4,1)S(1)} %copy-done.47), kind=kOutput, calls=%fused_computation.10 | convolution fusion | flops 303169536 | bytes 1667072 | tf_op jit(solution)/shard_map/transpose(jvp(hts,shp->thp))/dot_general | solution.py:380
  132.0 4.3 %fusion.7 = (f32[24,128]{1,0:T(8,128)}, f32[24,128]{1,0:T(8,128)}, f32[128,128]{1,0:T(8,128)S(1)}) fusion(f32[128,128]{1,0:T(8,128)S(1)} %copy-done.35, f32[24,128]{1,0:T(8,128)S(1)} %bitcast.96, pred[128,128]{1,0:T(8,128)(4,1)S(1)} %copy-done.48, f32[24,64,128]{2,1,0:T(8,128)S(1)} %bitcast.91, f32[128,24,64]{0,2,1:T(8,128)S(1)} %bitcast.88), kind=kOutput, calls=%fused_computation.22 | convolution fusion | flops 305506304 | bytes 1757184 | tf_op jit(solution)/shard_map/transpose(jvp(hts,shp->thp))/dot_general | solution.py:380
  136.9 2.3 copy.108
  139.1 21.6 %scan_back.1 = bf16[8,16,1536]{2,1,0:T(8,128)(2,1)} custom-call(bf16[8,16,1536]{2,1,0:T(8,128)(2,1)} %bitcast.86, f32[1,1536]{1,0:T(1,128)} %broadcast_in_dim_reshape.4.decay), custom_call_target="tpu_custom_call" | custom-call | tf_op jit(solution)/shard_map/scan_back/pallas_call | solution.py:328
  160.8 1.8 fusion.85
  162.6 1.1 convolution_add_fusion.1
  163.8 1.0 convolution_add_fusion.2
  164.9 4.3 %slice_multiply_fusion = (f32[128,1536]{1,0:T(8,128)}, f32[128,1536]{1,0:T(8,128)S(1)}, f32[128,1536]{1,0:T(8,128)}, f32[128,1536]{1,0:T(8,128)}) fusion(f32[128,1792]{1,0:T(8,128)} %copy-done, f32[128,1536]{1,0:T(8,128)} %copy.108, f32[128,1536]{1,0:T(8,128)S(1)} %copy-done.7, f32[128,1536]{1,0:T(8,128)S(1)} %copy-done.8, ...), kind=kOutput, calls=%fused_computation.68 | convolution fusion | flops 303562752 | bytes 9115648 | tf_op jit(solution)/shard_map/transpose(jvp())/dot_general | solution.py:384
  169.2 1.4 multiply_reduce_fusion.3
  172.5 2.3 convolution_convert_fusion.1
  174.8 1.7 collective-permute-start.1
  176.5 1.1 copy.110
  177.6 1.2 copy.113
  179.0 1.2 reduce_sum.232
  182.2 0.9 fusion.12
  183.4 4.2 %fusion.31 = (f32[768]{0:T(1024)S(1)}, f32[128]{0:T(128)S(1)}, f32[128,768]{1,0:T(8,128)S(1)}) fusion(bf16[128,768]{1,0:T(8,128)(2,1)S(1)} %copy-done.4, f32[128]{0:T(128)S(1)} %fusion.72, f32[768]{0:T(1024)S(1)} %copy-done.26, bf16[128,3456]{1,0:T(8,128)(2,1)S(1)} %concatenate.11, bf16[768,3456]{1,0:T(8,128)(2,1)} %bitcast.71), kind=kOutput, calls=%fused_computation.78 | convolution fusion | flops 680164480 | bytes 6790144 | tf_op jit(solution)/shard_map/dot_general | solution.py:417
  187.7 4.0 %convolution_convert_fusion = bf16[768,3456]{1,0:T(8,128)(2,1)} fusion(bf16[128,3456]{1,0:T(8,128)(2,1)S(1)} %concatenate.11, bf16[128,768]{1,0:T(8,128)(2,1)S(1)} %copy-done.4, f32[768]{0:T(1024)S(1)} %copy-done.26, f32[128]{0:T(128)S(1)} %fusion.72), kind=kOutput, calls=%fused_computation | convolution fusion | flops 682524672 | bytes 6393344 | tf_op jit(solution)/shard_map/dot_general | solution.py:411
  192.3 56.4 %sum_rows.1 = (f32[24,3456]{1,0:T(8,128)}, f32[24,1536]{1,0:T(8,128)}, f32[96,128]{1,0:T(8,128)}) custom-call(bf16[32,24,3456]{2,1,0:T(8,128)(2,1)} %bitcast.69, bf16[32,24,1536]{2,1,0:T(8,128)(2,1)} %bitcast.74, f32[96,128]{1,0:T(8,128)} %pad_bitcast_fusion.refs_2_), custom_call_target="tpu_custom_call" | custom-call | tf_op jit(solution)/shard_map/sum_rows/pallas_call | solution.py:254
  248.7 1.3 slice_bitcast_fusion.2
  250.1 0.8 slice.99
  250.8 1.3 slice_bitcast_fusion.1
  252.1 1.3 slice_bitcast_fusion
  254.1 1.4 fusion.83
  255.5 0.9 fusion.32
  256.4 0.7 copy.119
  (182 shorter events, 11.2 us)
Async XLA Ops:
  54.5 7.9 %copy-start.46 = (f32[1792,4]{0,1:T(4,128)S(1)}, f32[1792,4]{0,1:T(4,128)}, u32[]{:S(2)}) copy-start(f32[1792,4]{0,1:T(4,128)} %param.14) | copy-start | bytes 86020
  54.5 8.5 %copy-start.56 = (f32[24]{0:T(128)S(1)}, f32[24]{0:T(128)}, u32[]{:S(2)}) copy-start(f32[24]{0:T(128)} %param.17) | copy-start | bytes 292
  54.5 8.6 %copy-start.54 = (f32[24]{0:T(128)S(1)}, f32[24]{0:T(128)}, u32[]{:S(2)}) copy-start(f32[24]{0:T(128)} %param.16) | copy-start | bytes 292
  58.2 7.4 %copy-start.53 = (f32[24]{0:T(128)S(1)}, f32[24]{0:T(128)}, u32[]{:S(2)}) copy-start(f32[24]{0:T(128)} %param.18) | copy-start | bytes 292
  58.2 11.7 %collective-permute-start = (f32[3,1792]{1,0:T(4,128)S(1)}, f32[3,1792]{1,0:T(4,128)S(1)}, u32[]{:S(2)}, u32[]{:S(2)}) collective-permute-start(f32[3,1792]{1,0:T(4,128)S(1)} %slice.107), channel_id=1, source_target_pairs={{0,1},{1,2},{2,3},{3,4},{4,5},{5,6},{6,7},{8,9},{9,10},{10,11},{11... | collective-permute-start | bytes 64520 | tf_op jit(solution)/shard_map/ppermute | solution.py:350
  63.1 6.8 %copy-start.31 = (f32[1792]{0:T(1024)}, f32[1792]{0:T(1024)S(1)}, u32[]{:S(2)}) copy-start(f32[1792]{0:T(1024)S(1)} %get-tuple-element.35) | copy-start | bytes 21508
  64.0 2.6 %copy-start.29 = (f32[128,24]{0,1:T(8,128)}, f32[128,24]{0,1:T(8,128)S(1)}, u32[]{:S(2)}) copy-start(f32[128,24]{0,1:T(8,128)S(1)} %get-tuple-element.63) | copy-start | bytes 36868
  66.7 8.1 %copy-start.6 = (f32[128,1536]{1,0:T(8,128)}, f32[128,1536]{1,0:T(8,128)S(1)}, u32[]{:S(2)}) copy-start(f32[128,1536]{1,0:T(8,128)S(1)} %copy.102) | copy-start | bytes 2359300
  73.9 43.2 %copy-start = (f32[128,1792]{1,0:T(8,128)}, f32[128,1792]{1,0:T(8,128)S(1)}, u32[]{:S(2)}) copy-start(f32[128,1792]{1,0:T(8,128)S(1)} %get-tuple-element.47) | copy-start | bytes 2752516
  79.5 7.6 %copy-start.10 = (f32[128,1536]{1,0:T(8,128)S(1)}, f32[128,1536]{1,0:T(8,128)}, u32[]{:S(2)}) copy-start(f32[128,1536]{1,0:T(8,128)} %get-tuple-element.45) | copy-start | bytes 2359300
  84.9 32.2 %copy-start.41 = (f32[1536]{0:T(1024)S(1)}, f32[1536]{0:T(1024)}, u32[]{:S(2)}) copy-start(f32[1536]{0:T(1024)} %mul.363) | copy-start | bytes 18436
  117.1 3.3 %copy-start.2 = (bf16[32,24,1536]{2,1,0:T(8,128)(2,1)S(1)}, bf16[32,24,1536]{2,1,0:T(8,128)(2,1)}, u32[]{:S(2)}) copy-start(bf16[32,24,1536]{2,1,0:T(8,128)(2,1)} %get-tuple-element.17) | copy-start | bytes 7077892
  117.1 3.3 %copy-start.3 = (bf16[128,768]{1,0:T(8,128)(2,1)S(1)}, bf16[128,768]{1,0:T(8,128)(2,1)}, u32[]{:S(2)}) copy-start(bf16[128,768]{1,0:T(8,128)(2,1)} %param.11) | copy-start | bytes 589828
  117.1 3.3 %copy-start.28 = (f32[1536]{0:T(1024)S(1)}, f32[1536]{0:T(1024)}, u32[]{:S(2)}) copy-start(f32[1536]{0:T(1024)} %param.19) | copy-start | bytes 18436
  120.4 2.8 %copy-start.49 = (f32[128]{0:T(128)}, f32[128]{0:T(128)S(1)}, u32[]{:S(2)}) copy-start(f32[128]{0:T(128)S(1)} %fusion.73) | copy-start | bytes 1540
  125.2 4.1 %copy-start.35 = (f32[128,128]{1,0:T(8,128)S(1)}, f32[128,128]{1,0:T(8,128)}, u32[]{:S(2)}) copy-start(f32[128,128]{1,0:T(8,128)} %fusion.47) | copy-start | bytes 196612
  125.2 4.1 %copy-start.47 = (pred[128,128]{1,0:T(8,128)(4,1)S(1)}, pred[128,128]{1,0:T(8,128)(4,1)}, u32[]{:S(2)}) copy-start(pred[128,128]{1,0:T(8,128)(4,1)} %iota_compare_fusion) | copy-start | bytes 49156
  126.4 2.9 %copy-start.24 = (f32[128,1536]{0,1:T(8,128)S(1)}, f32[128,1536]{0,1:T(8,128)}, u32[]{:S(2)}) copy-start(f32[128,1536]{0,1:T(8,128)} %copy.106) | copy-start | bytes 2359300
  126.4 5.6 %copy-start.23 = (f32[128,1536]{0,1:T(8,128)S(1)}, f32[128,1536]{0,1:T(8,128)}, u32[]{:S(2)}) copy-start(f32[128,1536]{0,1:T(8,128)} %copy.101) | copy-start | bytes 2359300
  126.4 5.6 %copy-start.48 = (pred[128,128]{1,0:T(8,128)(4,1)S(1)}, pred[128,128]{1,0:T(8,128)(4,1)}, u32[]{:S(2)}) copy-start(pred[128,128]{1,0:T(8,128)(4,1)} %iota_compare_fusion) | copy-start | bytes 49156
  132.0 4.3 %copy-start.9 = (f32[128,1536]{1,0:T(8,128)S(1)}, f32[128,1536]{1,0:T(8,128)}, u32[]{:S(2)}) copy-start(f32[128,1536]{1,0:T(8,128)} %copy.103) | copy-start | bytes 2359300
  132.0 4.3 %copy-start.13 = (bf16[8,16,1536]{2,1,0:T(8,128)(2,1)S(1)}, bf16[8,16,1536]{2,1,0:T(8,128)(2,1)}, u32[]{:S(2)}) copy-start(bf16[8,16,1536]{2,1,0:T(8,128)(2,1)} %scan_states.1) | copy-start | bytes 1179652
  160.8 4.0 %copy-start.7 = (f32[128,1536]{1,0:T(8,128)S(1)}, f32[128,1536]{1,0:T(8,128)}, u32[]{:S(2)}) copy-start(f32[128,1536]{1,0:T(8,128)} %copy-done.6) | copy-start | bytes 2359300
  160.8 4.0 %copy-start.8 = (f32[128,1536]{1,0:T(8,128)S(1)}, f32[128,1536]{1,0:T(8,128)}, u32[]{:S(2)}) copy-start(f32[128,1536]{1,0:T(8,128)} %copy.100) | copy-start | bytes 2359300
  164.8 4.3 %copy-start.5 = (f32[128,1792]{1,0:T(8,128)S(1)}, f32[128,1792]{1,0:T(8,128)}, u32[]{:S(2)}) copy-start(f32[128,1792]{1,0:T(8,128)} %slice.108) | copy-start | bytes 2752516
  164.8 4.3 %copy-start.12 = (f32[128,1792]{1,0:T(8,128)S(1)}, f32[128,1792]{1,0:T(8,128)}, u32[]{:S(2)}) copy-start(f32[128,1792]{1,0:T(8,128)} %get-tuple-element.48) | copy-start | bytes 2752516
  172.4 4.0 %copy-start.17 = (f32[128,1536]{1,0:T(8,128)S(1)}, f32[128,1536]{1,0:T(8,128)}, u32[]{:S(2)}) copy-start(f32[128,1536]{1,0:T(8,128)} %get-tuple-element.50) | copy-start | bytes 2359300
  174.8 2.8 %copy-start.16 = (f32[128,1536]{1,0:T(8,128)S(1)}, f32[128,1536]{1,0:T(8,128)}, u32[]{:S(2)}) copy-start(f32[128,1536]{1,0:T(8,128)} %get-tuple-element.57) | copy-start | bytes 2359300
  174.8 7.4 %collective-permute-start.1 = (f32[3,1792]{1,0:T(4,128)}, f32[3,1792]{1,0:T(4,128)}, u32[]{:S(2)}, u32[]{:S(2)}) collective-permute-start(f32[3,1792]{1,0:T(4,128)} %pad_add_fusion.1), channel_id=1, source_target_pairs={{1,0},{2,1},{3,2},{4,3},{5,4},{6,5},{7,6},{9,8},{10,9},{11,10},{12... | collective-permute-start | bytes 64520 | tf_op jit(solution)/shard_map/ppermute | solution.py:350
  177.6 2.6 %copy-start.30 = (f32[128,24]{0,1:T(8,128)S(1)}, f32[128,24]{0,1:T(8,128)}, u32[]{:S(2)}) copy-start(f32[128,24]{0,1:T(8,128)} %copy-done.29) | copy-start | bytes 36868
  177.6 2.9 %copy-start.15 = (f32[128,1536]{1,0:T(8,128)S(1)}, f32[128,1536]{1,0:T(8,128)}, u32[]{:S(2)}) copy-start(f32[128,1536]{1,0:T(8,128)} %get-tuple-element.56) | copy-start | bytes 2359300
  178.9 2.4 copy-start.45
  178.9 2.4 copy-start.44
  178.9 2.4 copy-start.43
  178.9 2.5 copy-start.42
  178.9 2.5 copy-start.37
  178.9 2.5 copy-start.55
  178.9 2.5 copy-start.59
  178.9 2.5 copy-start.60
  179.0 2.5 copy-start.61
  179.0 2.5 copy-start.62
  180.7 2.4 copy-start.22
  187.6 4.0 %copy-start.38 = (f32[1536]{0:T(1024)S(1)}, f32[1536]{0:T(1024)}, u32[]{:S(2)}) copy-start(f32[1536]{0:T(1024)} %get-tuple-element.27) | copy-start | bytes 18436
  187.7 4.0 %copy-start.39 = (f32[1792]{0:T(1024)S(1)}, f32[1792]{0:T(1024)}, u32[]{:S(2)}) copy-start(f32[1792]{0:T(1024)} %get-tuple-element.29) | copy-start | bytes 21508
  192.3 61.1 %copy-start.52 = (f32[128]{0:T(128)S(1)}, f32[128]{0:T(128)}, u32[]{:S(2)}) copy-start(f32[128]{0:T(128)} %copy-done.51) | copy-start | bytes 1540
  192.3 63.1 %copy-start.21 = (bf16[128,768]{1,0:T(8,128)(2,1)S(1)}, bf16[128,768]{1,0:T(8,128)(2,1)}, u32[]{:S(2)}) copy-start(bf16[128,768]{1,0:T(8,128)(2,1)} %param.21) | copy-start | bytes 589828
  248.7 7.7 %copy-start.25 = (f32[24,3456]{1,0:T(8,128)S(1)}, f32[24,3456]{1,0:T(8,128)}, u32[]{:S(2)}) copy-start(f32[24,3456]{1,0:T(8,128)} %get-tuple-element.18) | copy-start | bytes 995332
  248.7 8.4 %copy-start.27 = (f32[24,1536]{1,0:T(8,128)S(1)}, f32[24,1536]{1,0:T(8,128)}, u32[]{:S(2)}) copy-start(f32[24,1536]{1,0:T(8,128)} %get-tuple-element.85) | copy-start | bytes 442372
  (17 other events, 20.9 us)

commit v2 on v1

--- a/solution.py
+++ b/solution.py
@@ -273,7 +273,100 @@
     )(*terms, vector)
 
 
-def scan_kernel(count, reverse, state, decay, out, came, came_decay, ready, *sems):
+GROUP = 4
+GROUP_LANES = GROUP * HEAD_DIM
+
+
+def inner_product(left, right, dims):
+    return lax.dot_general(
+        left, right, (dims, ((), ())), precision=HIGH, preferred_element_type=jnp.float32
+    )
+
+
+def group_lanes(group):
+    return pl.ds(pl.multiple_of(group * GROUP_LANES, GROUP_LANES), GROUP_LANES)
+
+
+def head_weights(cumulative, head):
+    row = cumulative[pl.ds(head, 1), :]
+    count = row.shape[1]
+    spread = jnp.broadcast_to(row, (count, count))
+    later = lax.broadcasted_iota(jnp.int32, (count, count), 0)
+    earlier = lax.broadcasted_iota(jnp.int32, (count, count), 1)
+    return jnp.exp(jnp.where(later >= earlier, spread.T - spread, -jnp.inf))
+
+
+def inside_work(first, last, scaled_x, b_mat, c_mat, cumulative, output, crossed):
+    if first == 0:
+        crossed[...] = inner_product(c_mat[...], b_mat[...], ((1,), (1,)))
+
+    def one(group, carry):
+        values = scaled_x[:, group_lanes(group)]
+        parts = []
+        for i in range(GROUP):
+            scores = head_weights(cumulative, group * GROUP + i) * crossed[...]
+            head = values[:, i * HEAD_DIM : (i + 1) * HEAD_DIM]
+            parts.append(inner_product(scores, head, ((1,), (0,))))
+        output[:, group_lanes(group)] = jnp.concatenate(parts, axis=1)
+        return carry
+
+    lax.fori_loop(first, last, one, 0)
+
+
+def inside_back(
+    first,
+    last,
+    output_cot,
+    scaled_x,
+    b_mat,
+    c_mat,
+    cumulative,
+    scaled_cot,
+    b_cot,
+    c_cot,
+    cumulative_cot,
+    crossed,
+    crossed_cot,
+):
+    if first == 0:
+        crossed[...] = inner_product(c_mat[...], b_mat[...], ((1,), (1,)))
+        crossed_cot[...] = jnp.zeros_like(crossed_cot)
+
+    def one(group, carry):
+        values = scaled_x[:, group_lanes(group)]
+        cots = output_cot[:, group_lanes(group)]
+        parts = []
+        total = crossed_cot[...]
+        for i in range(GROUP):
+            weights = head_weights(cumulative, group * GROUP + i)
+            scores = weights * crossed[...]
+            head = values[:, i * HEAD_DIM : (i + 1) * HEAD_DIM]
+            cot = cots[:, i * HEAD_DIM : (i + 1) * HEAD_DIM]
+            weighted = weights * inner_product(cot, head, ((1,), (1,)))
+            total = total + weighted
+            parts.append(inner_product(scores, cot, ((0,), (0,))))
+            moved = weighted * crossed[...]
+            cumulative_cot[pl.ds(group * GROUP + i, 1), :] = jnp.sum(
+                moved.T, axis=0, keepdims=True
+            ) - jnp.sum(moved, axis=0, keepdims=True)
+        crossed_cot[...] = total
+        scaled_cot[:, group_lanes(group)] = jnp.concatenate(parts, axis=1)
+        return carry
+
+    lax.fori_loop(first, last, one, 0)
+    if last == HEADS // GROUP:
+        b_cot[...] = inner_product(crossed_cot[...], c_mat[...], ((0,), (0,)))
+        c_cot[...] = inner_product(crossed_cot[...], b_mat[...], ((1,), (0,)))
+
+
+def scan_kernel(count, reverse, work, inputs, outputs, *refs):
+    state, decay = refs[:2]
+    given = refs[2 : 2 + inputs]
+    out = refs[2 + inputs]
+    made = refs[3 + inputs : 3 + inputs + outputs]
+    came, came_decay, ready = refs[3 + inputs + outputs : 6 + inputs + outputs]
+    sems = refs[6 + inputs + outputs : 12 + inputs + outputs]
+    held = refs[12 + inputs + outputs :]
     out_send, out_recv, decay_send, decay_recv, back_send, back_recv = sems
     dp_at, seq_at = places()
     barrier = pltpu.get_barrier_semaphore()
@@ -303,6 +396,8 @@
         copy(hop, 1).start()
     came[seq_at] = state[seq_at]
     came_decay[seq_at] = decay[...]
+    groups = HEADS // GROUP
+    work(0, groups // 2, *given, *made, *held)
     for hop in range(1, count):
         copy(hop, 0).wait_recv()
         copy(hop, 1).wait_recv()
@@ -313,6 +408,7 @@
     for hop in range(1, count):
         copy(hop, 2).start()
     out[seq_at] = ready[seq_at]
+    work(groups // 2, groups, *given, *made, *held)
     for hop in range(1, count):
         copy(hop, 2).wait_recv()
     for hop in range(1, count):
@@ -320,28 +416,29 @@
             copy(hop, which).wait_send()
 
 
-def scan_states(state, decay, reverse, collective_id):
+def scan_states(state, decay, work, given, made, held, reverse, collective_id):
     count = lax.axis_size("seq")
     state = state.astype(jnp.bfloat16).reshape(count, STATE // count, DI)
     in_vmem = pl.BlockSpec(memory_space=pltpu.VMEM)
-    sems = [pltpu.SemaphoreType.DMA((count,))] * 6
     got = pl.pallas_call(
-        partial(scan_kernel, count, reverse),
-        out_shape=jax.ShapeDtypeStruct(state.shape, state.dtype),
-        in_specs=[in_vmem, in_vmem],
-        out_specs=in_vmem,
+        partial(scan_kernel, count, reverse, work, len(given), len(made)),
+        out_shape=[jax.ShapeDtypeStruct(state.shape, state.dtype)]
+        + [jax.ShapeDtypeStruct(shape, jnp.float32) for shape in made],
+        in_specs=[in_vmem] * (2 + len(given)),
+        out_specs=[in_vmem] * (1 + len(made)),
         scratch_shapes=[
             pltpu.VMEM(state.shape, state.dtype),
             pltpu.VMEM((count, 1, DI), jnp.float32),
             pltpu.VMEM(state.shape, state.dtype),
         ]
-        + sems,
+        + [pltpu.SemaphoreType.DMA((count,))] * 6
+        + [pltpu.VMEM(shape, jnp.float32) for shape in held],
         compiler_params=pltpu.CompilerParams(
             collective_id=collective_id, has_side_effects=True, vmem_limit_bytes=VMEM_BYTES
         ),
         name="scan_back" if reverse else "scan_states",
-    )(state, decay[None, :])
-    return got.reshape(STATE, DI).astype(jnp.float32)
+    )(state, decay[None, :], *given)
+    return got[0].reshape(STATE, DI).astype(jnp.float32), *got[1:]
 
 
 def passed_along(value, axis, steps):
@@ -366,26 +463,7 @@
     return jnp.repeat(by_head, HEAD_DIM, axis=-1)
 
 
-def ssd_block(xs, b_block, c_block, step_block, decay_block):
-    row_count = xs.shape[0]
-    at = jnp.arange(row_count)
-    lower = at[:, None] >= at[None, :]
-    cumulative = jnp.dot(lower.astype(jnp.float32), decay_block, precision=HIGH)
-    by_head = cumulative.T
-    spread = by_head[:, :, None] - by_head[:, None, :]
-    weights_mat = jnp.exp(jnp.where(lower[None], spread, -jnp.inf))
-    intersection = jnp.dot(c_block, b_block.T, precision=HIGH)
-    scaled_x = xs * spread_heads(step_block)
-    scores = weights_mat * intersection[None]
-    output = jnp.einsum(
-        "hts,shp->thp", scores, scaled_x.reshape(row_count, HEADS, HEAD_DIM), precision=HIGH
-    )
-    tail = jnp.exp(cumulative[-1][None, :] - cumulative)
-    fresh = jnp.dot(b_block.T, scaled_x * spread_heads(tail), precision=HIGH)
-    return output.reshape(row_count, DI), cumulative, fresh
-
-
-def mid_local(xbc, dt_raw, edge, conv_weight, conv_bias, dt_bias, a_log):
+def before_states(xbc, dt_raw, edge, conv_weight, conv_bias, dt_bias, a_log):
     row_count = xbc.shape[0]
     activated = conv_silu(jnp.concatenate([edge, xbc], axis=0), conv_weight, conv_bias, row_count)
     xs = activated[:, :DI]
@@ -393,8 +471,13 @@
     c_mat = activated[:, DI + STATE :]
     step = jax.nn.softplus(dt_raw + dt_bias)
     log_decay = step * -jnp.exp(a_log)
-    ssd_out, cumulative, final = ssd_block(xs, b_mat, c_mat, step, log_decay)
-    return (ssd_out, xs, c_mat, cumulative, final)
+    at = jnp.arange(row_count)
+    lower = (at[:, None] >= at[None, :]).astype(jnp.float32)
+    cumulative = jnp.dot(lower, log_decay, precision=HIGH)
+    scaled_x = xs * spread_heads(step)
+    tail = jnp.exp(cumulative[-1][None, :] - cumulative)
+    fresh = jnp.dot(b_mat.T, scaled_x * spread_heads(tail), precision=HIGH)
+    return (xs, scaled_x, b_mat, c_mat, cumulative, fresh)
 
 
 def post_gate(ssd_out, xs, gate_part, skip_gain, gated_gain):
@@ -447,12 +530,23 @@
     dt_raw = projected[:, DI + XBC : PROJ]
     edge = passed_along(xbc[row_count - (CONV - 1) :], "seq", 1)
     primal, mid_back = jax.vjp(
-        mid_local, xbc, dt_raw, edge, conv_weight, conv_bias, dt_bias, a_log
-    )
-    local_out, xs, c_mat, cumulative, s_local = primal
+        before_states, xbc, dt_raw, edge, conv_weight, conv_bias, dt_bias, a_log
+    )
+    xs, scaled_x, b_mat, c_mat, cumulative, s_local = primal
+    by_head = cumulative.T
     decay = jnp.exp(cumulative[-1])
     wide_decay = spread_heads(decay)
-    state_in = scan_states(s_local, wide_decay, False, collective_id=2)
+    square = (row_count, row_count)
+    state_in, local_out = scan_states(
+        s_local,
+        wide_decay,
+        inside_work,
+        [scaled_x, b_mat, c_mat, by_head],
+        [xs.shape],
+        [square],
+        False,
+        collective_id=2,
+    )
     weighted = spread_heads(jnp.exp(cumulative))
     carried_part = jnp.dot(c_mat, state_in, precision=HIGH) * weighted
     ssd_out = local_out + carried_part
@@ -464,13 +558,24 @@
     ssd_cot, xs_cot, gate_cot, skip_grad, gated_gain_grad = post_back(gated_cot)
     scaled_cot = ssd_cot * weighted
     local_grad = jnp.dot(c_mat.T, scaled_cot, precision=HIGH)
-    later_grad = scan_states(local_grad, wide_decay, True, collective_id=3)
+    later_grad, scaled_x_cot, b_cot, inner_c_cot, by_head_cot = scan_states(
+        local_grad,
+        wide_decay,
+        inside_back,
+        [ssd_cot, scaled_x, b_mat, c_mat, by_head],
+        [xs.shape, b_mat.shape, c_mat.shape, by_head.shape],
+        [square, square],
+        True,
+        collective_id=3,
+    )
     c_cot = lax.dot_general(scaled_cot, state_in, (((1,), (1,)), ((), ())), precision=HIGH)
     cum_cot = jnp.sum((ssd_cot * carried_part).reshape(row_count, HEADS, HEAD_DIM), axis=2)
     last_cot = jnp.sum(later_grad * state_in, axis=0).reshape(HEADS, HEAD_DIM).sum(axis=1) * decay
     is_last = (jnp.arange(row_count) == row_count - 1)[:, None]
     cum_cot = cum_cot + jnp.where(is_last, last_cot[None, :], 0.0)
-    mid_grads = mid_back((ssd_cot, xs_cot, c_cot, cum_cot, later_grad))
+    mid_grads = mid_back(
+        (xs_cot, scaled_x_cot, b_cot, c_cot + inner_c_cot, cum_cot + by_head_cot.T, later_grad)
+    )
     xbc_cot, dt_cot, edge_cot, conv_weight_grad, conv_bias_grad, dt_bias_grad, a_log_grad = (
         mid_grads
     )

time: 259 us -> 250 us (0.965)
  matrix products: 47.1 us -> 32.8 us
  local copies, waits for them, and re-layouts: 29.6 us -> 33.8 us
    dot_general x11 -> x5, matrix products: 23.7 us -> 9 us  [the longest x3 7.35 us: before_states(): fresh = jnp.dot(b_mat.T, scaled_x * spread_heads(tail), precision=HIGH)]
    reshape x3 -> x0, local copies, waits for them, and re-layouts: 4.68 us -> none  [the longest x1 2.3 us: ssd_block(): return (output.reshape(row_count, DI), cumulative, fresh)]
    reshape x3, local copies, waits for them, and re-layouts: 2.58 us -> 6.84 us  [spread_heads(): return jnp.repeat(by_head, HEAD_DIM, axis=-1)]
    mul x4 -> x2, local copies, waits for them, and re-layouts: 5.81 us -> 2.67 us  [the longest x1 1.42 us: before_states(): scaled_x = xs * spread_heads(step)]
    broadcast_in_dim x4, local copies, waits for them, and re-layouts: 0.23 us -> 3.08 us  [spread_heads(): return jnp.repeat(by_head, HEAD_DIM, axis=-1)]
  transfers between devices with their start and end apart: 2 -> 2, of which waited for: 0 -> 0; matrix products, arithmetic and copies ran while one was open for 5% -> 10% of each run, Pallas kernels for 0% -> 0%
where the time goes in v2:
time: 250 us; the launch traced here: 249 us
  Pallas kernels  159 us (64%)
  local copies, waits for them, and re-layouts  33.8 us (14%)
  matrix products  32.8 us (13%)
  other arithmetic  16.9 us (7%)
  starting transfers between devices  4.92 us (2%)
    pallas_call x1, Pallas kernels, sum_to_owners(): pl.pallas_call(partial(sum_kernel, seq_bits, streams, bits, len(terms)),...  56.4 us
    pallas_call x2, Pallas kernels, scan_states(): pl.pallas_call(partial(scan_kernel, count, reverse, work, len(given), len...  51.5 us
    pallas_call x1, Pallas kernels, gather_all(): pl.pallas_call(partial(gather_kernel, seq_bits, streams, bits), out_shape...  50.7 us
    dot_general x3, matrix products, before_states(): fresh = jnp.dot(b_mat.T, scaled_x * spread_heads(tail), precision=HIGH)  7.35 us
    reshape x3, local copies, waits for them, and re-layouts, spread_heads(): return jnp.repeat(by_head, HEAD_DIM, axis=-1)  6.84 us
    dot_general x2, matrix products, contract_rows(): lax.dot_general(left, right, (((0,), (0,)), ((), ())), preferred_element_...  6.27 us
    slice x5, local copies, waits for them, and re-layouts, body(): parts.append(summed[at:at + a.size].reshape(a.shape))  6.02 us
    dot_general x2, matrix products, contract_cols(): lax.dot_general(left, right, (((1,), (1,)), ((), ())), preferred_element_...  5.83 us
  transfers between devices with their start and end apart: 2, of which 0 were waited for; matrix products, arithmetic and copies ran while one was open for 10% of the time, Pallas kernels for 0%

profile of v2, /device:TPU:0, one launch (start us, length us, event | category | flops | bytes accessed | tf_op | source)
XLA Modules:
  0.0 248.6 jit_solution(17665794755876395268)
XLA Ops:
  0.6 1.0 fusion.16
  2.3 1.6 pad.48.refs_0_
  3.9 50.7 %gather_rows.1 = (bf16[32,24,3456]{2,1,0:T(8,128)(2,1)}, bf16[32,24,1536]{2,1,0:T(8,128)(2,1)}) custom-call(bf16[24,3456]{1,0:T(8,128)(2,1)} %pad.48.refs_0_, bf16[24,1536]{1,0:T(8,128)(2,1)} %refs_1_.1), custom_call_target="tpu_custom_call" | custom-call | tf_op jit(solution)/shard_map/gather_rows/pallas_call | solution.py:134
  54.6 3.6 %fusion.36 = f32[128,3456]{1,0:T(8,128)S(1)} fusion(bf16[768,3456]{1,0:T(8,128)(2,1)} %bitcast.58, bf16[128,768]{1,0:T(8,128)(2,1)} %param.11, f32[768]{0:T(1024)} %param.12, f32[128]{0:T(128)S(1)} %fusion.43), kind=kOutput, calls=%fused_computation.88 | convolution fusion | flops 679870464 | bytes 7278080 | tf_op jit(solution)/shard_map/dot_general | solution.py:527
  58.3 3.4 %collective-permute-start = (f32[3,1792]{1,0:T(4,128)S(1)}, f32[3,1792]{1,0:T(4,128)S(1)}, u32[]{:S(2)}, u32[]{:S(2)}) collective-permute-start(f32[3,1792]{1,0:T(4,128)S(1)} %slice.107), channel_id=1, source_target_pairs={{0,1},{1,2},{2,3},{3,4},{4,5},{5,6},{6,7},{8,9},{9,10},{10,11},{11... | collective-permute-start | bytes 64520 | tf_op jit(solution)/shard_map/ppermute | solution.py:447
  64.1 1.0 broadcast_in_dim.67
  65.1 2.3 copy.87
  67.4 1.0 broadcast_in_dim.66
  68.4 2.3 copy.83
  71.4 1.0 broadcast_in_dim.69
  72.4 2.3 copy.88
  74.7 1.6 fusion.6
  77.0 2.5 fusion.56
  79.5 1.6 convolution_convert_fusion.3
  81.1 28.9 %scan_states.1 = (bf16[8,16,1536]{2,1,0:T(8,128)(2,1)}, f32[128,1536]{1,0:T(8,128)}) custom-call(bf16[8,16,1536]{2,1,0:T(8,128)(2,1)} %bitcast.74, f32[1,1536]{1,0:T(1,128)} %broadcast_in_dim_reshape.4.refs_1_, f32[128,1536]{1,0:T(8,128)} %get-tuple-element.57.refs_2_.refs_3_, f32[128,128]{1,0:T(8,128)} %get-tuple-element.68.refs_3_.refs_4_, ...), custom_call_target="tpu_custom_call" | custom-call | tf_op jit(solution)/shard_map/scan_states/pallas_call | solution.py:423
  110.1 3.3 %multiply_reduce_fusion.8 = (f32[128]{0:T(128)S(1)}, f32[128,1536]{1,0:T(8,128)S(1)}, f32[128,1536]{1,0:T(8,128)S(1)}, f32[128,1536]{1,0:T(8,128)}) fusion(f32[128,3456]{1,0:T(8,128)S(1)} %fusion.36, f32[1536]{0:T(1024)} %mul.341, f32[128,1792]{1,0:T(8,128)S(1)} %get-tuple-element.58, f32[128,1536]{1,0:T(8,128)} %get-tuple-element.24, ...), kind=kOutput, calls=%fused_computation.42 | convolution fusion | flops 304152448 | bytes 5970432 | tf_op jit(solution)/shard_map/dot_general | solution.py:551
  113.4 1.6 fusion
  115.0 1.1 multiply_reduce_fusion.5
  116.2 1.9 multiply_reduce_fusion.4
  118.1 1.6 convolution_convert_fusion.2
  119.7 22.6 %scan_back.1 = (bf16[8,16,1536]{2,1,0:T(8,128)(2,1)}, f32[128,1536]{1,0:T(8,128)}, f32[128,128]{1,0:T(8,128)}, f32[128,128]{1,0:T(8,128)}, f32[24,128]{1,0:T(8,128)}) custom-call(bf16[8,16,1536]{2,1,0:T(8,128)(2,1)} %bitcast.73, f32[1,1536]{1,0:T(1,128)} %broadcast_in_dim_reshape.4.refs_1_, f32[128,1536]{1,0:T(8,128)} %copy-done, ...), custom_call_target="tpu_custom_call" | custom-call | tf_op jit(solution)/shard_map/scan_back/pallas_call | solution.py:423
  142.4 2.1 convolution_add_fusion.2
  144.5 1.8 convolution_add_fusion.1
  146.4 4.0 %slice_multiply_fusion = (f32[128,1536]{1,0:T(8,128)}, f32[128,1536]{1,0:T(8,128)S(1)}, f32[128,1536]{1,0:T(8,128)}, f32[128,1536]{1,0:T(8,128)}) fusion(f32[128,1792]{1,0:T(8,128)} %copy-done.6, f32[128,1536]{1,0:T(8,128)} %get-tuple-element.30, f32[128,1536]{1,0:T(8,128)S(1)} %copy-done.10, f32[128,1536]{1,0:T(8,128)S(1)} %copy-done.11, ...), kind=kOutput, calls=%fused_computation.50 | convolution fusion | flops 303562752 | bytes 9115648 | tf_op jit(solution)/shard_map/transpose(jvp())/dot_general | solution.py:479
  150.4 1.4 multiply_reduce_fusion.2
  152.2 1.3 pad_add_fusion
  155.2 2.3 convolution_convert_fusion.1
  157.5 1.5 collective-permute-start.1
  159.0 1.4 copy.92
  160.6 0.8 copy.96
  161.6 1.3 copy.97
  162.8 1.3 reduce_sum.204
  164.3 2.4 copy.93
  166.7 1.2 reduce_sum.197
  168.7 1.4 fusion.52
  170.3 0.8 fusion.5
  171.2 1.2 concatenate.11
  172.4 4.2 %fusion.14 = (f32[768]{0:T(1024)S(1)}, f32[128]{0:T(128)S(1)}, f32[128,768]{1,0:T(8,128)S(1)}) fusion(bf16[128,768]{1,0:T(8,128)(2,1)S(1)} %copy-done.5, f32[128]{0:T(128)} %copy-done.53, f32[768]{0:T(1024)S(1)} %copy-done.30, bf16[128,3456]{1,0:T(8,128)(2,1)S(1)} %concatenate.11, bf16[768,3456]{1,0:T(8,128)(2,1)} %bitcast.59), kind=kOutput, calls=%fused_computation.60 | convolution fusion | flops 680164480 | bytes 6790144 | tf_op jit(solution)/shard_map/dot_general | solution.py:500
  176.7 4.0 %convolution_convert_fusion = bf16[768,3456]{1,0:T(8,128)(2,1)} fusion(bf16[128,3456]{1,0:T(8,128)(2,1)S(1)} %concatenate.11, bf16[128,768]{1,0:T(8,128)(2,1)S(1)} %copy-done.5, f32[768]{0:T(1024)S(1)} %copy-done.30, f32[128]{0:T(128)S(1)} %copy-done.54), kind=kOutput, calls=%fused_computation | convolution fusion | flops 682524672 | bytes 6393344 | tf_op jit(solution)/shard_map/dot_general | solution.py:494
  181.4 56.4 %sum_rows.1 = (f32[24,3456]{1,0:T(8,128)}, f32[24,1536]{1,0:T(8,128)}, f32[96,128]{1,0:T(8,128)}) custom-call(bf16[32,24,3456]{2,1,0:T(8,128)(2,1)} %bitcast.57, bf16[32,24,1536]{2,1,0:T(8,128)(2,1)} %bitcast.62, f32[96,128]{1,0:T(8,128)} %pad_bitcast_fusion.refs_2_), custom_call_target="tpu_custom_call" | custom-call | tf_op jit(solution)/shard_map/sum_rows/pallas_call | solution.py:254
  237.7 1.3 slice_bitcast_fusion.2
  239.0 0.8 slice.99
  239.8 1.3 slice_bitcast_fusion.1
  241.1 1.3 slice_bitcast_fusion
  243.0 1.4 fusion.58
  244.4 0.9 fusion.15
  245.3 1.7 copy.106
  247.0 1.6 copy.107
  (191 shorter events, 9.0 us)
Async XLA Ops:
  2.3 55.9 %copy-start.53 = (f32[128]{0:T(128)}, f32[128]{0:T(128)S(1)}, u32[]{:S(2)}) copy-start(f32[128]{0:T(128)S(1)} %fusion.43) | copy-start | bytes 1540
  54.6 7.1 %copy-start.60 = (f32[24]{0:T(128)S(1)}, f32[24]{0:T(128)}, u32[]{:S(2)}) copy-start(f32[24]{0:T(128)} %param.16) | copy-start | bytes 292
  54.6 7.1 %copy-start.69 = (f32[24]{0:T(128)S(1)}, f32[24]{0:T(128)}, u32[]{:S(2)}) copy-start(f32[24]{0:T(128)} %param.17) | copy-start | bytes 292
  54.6 7.7 %copy-start.52 = (f32[1792,4]{0,1:T(4,128)S(1)}, f32[1792,4]{0,1:T(4,128)}, u32[]{:S(2)}) copy-start(f32[1792,4]{0,1:T(4,128)} %param.14) | copy-start | bytes 86020
  58.2 5.0 %copy-start.68 = (f32[24]{0:T(128)S(1)}, f32[24]{0:T(128)}, u32[]{:S(2)}) copy-start(f32[24]{0:T(128)} %param.18) | copy-start | bytes 292
  58.3 16.4 %collective-permute-start = (f32[3,1792]{1,0:T(4,128)S(1)}, f32[3,1792]{1,0:T(4,128)S(1)}, u32[]{:S(2)}, u32[]{:S(2)}) collective-permute-start(f32[3,1792]{1,0:T(4,128)S(1)} %slice.107), channel_id=1, source_target_pairs={{0,1},{1,2},{2,3},{3,4},{4,5},{5,6},{6,7},{8,9},{9,10},{10,11},{11... | collective-permute-start | bytes 64520 | tf_op jit(solution)/shard_map/ppermute | solution.py:447
  61.8 5.6 %copy-start.22 = (f32[128,24]{1,0:T(8,128)}, f32[128,24]{1,0:T(8,128)S(1)}, u32[]{:S(2)}) copy-start(f32[128,24]{1,0:T(8,128)S(1)} %compare_select_fusion.2) | copy-start | bytes 36868
  62.0 6.4 %copy-start.28 = (f32[128,24]{0,1:T(8,128)}, f32[128,24]{0,1:T(8,128)S(1)}, u32[]{:S(2)}) copy-start(f32[128,24]{0,1:T(8,128)S(1)} %get-tuple-element.76) | copy-start | bytes 36868
  62.1 6.3 %copy-start.26 = (f32[128,24]{1,0:T(8,128)}, f32[128,24]{1,0:T(8,128)S(1)}, u32[]{:S(2)}) copy-start(f32[128,24]{1,0:T(8,128)S(1)} %copy.85) | copy-start | bytes 36868
  62.4 12.2 %copy-start.35 = (f32[1792]{0:T(1024)}, f32[1792]{0:T(1024)S(1)}, u32[]{:S(2)}) copy-start(f32[1792]{0:T(1024)S(1)} %get-tuple-element.44) | copy-start | bytes 21508
  62.5 12.2 %copy-start.37 = (f32[1792]{0:T(1024)}, f32[1792]{0:T(1024)S(1)}, u32[]{:S(2)}) copy-start(f32[1792]{0:T(1024)S(1)} %get-tuple-element.45) | copy-start | bytes 21508
  62.5 12.2 %copy-start.39 = (f32[1792]{0:T(1024)}, f32[1792]{0:T(1024)S(1)}, u32[]{:S(2)}) copy-start(f32[1792]{0:T(1024)S(1)} %get-tuple-element.46) | copy-start | bytes 21508
  62.5 12.2 %copy-start.41 = (f32[1792]{0:T(1024)}, f32[1792]{0:T(1024)S(1)}, u32[]{:S(2)}) copy-start(f32[1792]{0:T(1024)S(1)} %get-tuple-element.47) | copy-start | bytes 21508
  62.5 5.9 %copy-start.24 = (f32[128,24]{1,0:T(8,128)}, f32[128,24]{1,0:T(8,128)S(1)}, u32[]{:S(2)}) copy-start(f32[128,24]{1,0:T(8,128)S(1)} %subtract_exponential_fusion) | copy-start | bytes 36868
  63.1 11.6 %copy-start.8 = (f32[128,1792]{1,0:T(8,128)}, f32[128,1792]{1,0:T(8,128)S(1)}, u32[]{:S(2)}) copy-start(f32[128,1792]{1,0:T(8,128)S(1)} %slice.108) | copy-start | bytes 2752516
  67.4 7.3 %copy-start.55 = (f32[1792]{0:T(1024)S(1)}, f32[1792]{0:T(1024)}, u32[]{:S(2)}) copy-start(f32[1792]{0:T(1024)} %param.15) | copy-start | bytes 21508
  74.7 4.8 %copy-start.33 = (f32[3,1792]{1,0:T(4,128)}, f32[3,1792]{1,0:T(4,128)S(1)}, u32[]{:S(2)}) copy-start(f32[3,1792]{1,0:T(4,128)S(1)} %collective-permute-done) | copy-start | bytes 64516
  76.3 33.7 %copy-start.6 = (f32[128,1792]{1,0:T(8,128)}, f32[128,1792]{1,0:T(8,128)S(1)}, u32[]{:S(2)}) copy-start(f32[128,1792]{1,0:T(8,128)S(1)} %get-tuple-element.58) | copy-start | bytes 2752516
  79.5 30.5 %copy-start.13 = (f32[128,1536]{1,0:T(8,128)}, f32[128,1536]{1,0:T(8,128)S(1)}, u32[]{:S(2)}) copy-start(f32[128,1536]{1,0:T(8,128)S(1)} %get-tuple-element.56) | copy-start | bytes 2359300
  119.7 26.6 %copy-start.2 = (f32[128,1536]{1,0:T(8,128)S(1)}, f32[128,1536]{1,0:T(8,128)}, u32[]{:S(2)}) copy-start(f32[128,1536]{1,0:T(8,128)} %get-tuple-element.57.refs_2_.refs_3_) | copy-start | bytes 2359300
  146.3 4.1 %copy-start.9 = (f32[128,1792]{1,0:T(8,128)S(1)}, f32[128,1792]{1,0:T(8,128)}, u32[]{:S(2)}) copy-start(f32[128,1792]{1,0:T(8,128)} %copy-done.8) | copy-start | bytes 2752516
  146.4 4.1 %copy-start.15 = (f32[128,1792]{1,0:T(8,128)S(1)}, f32[128,1792]{1,0:T(8,128)}, u32[]{:S(2)}) copy-start(f32[128,1792]{1,0:T(8,128)} %get-tuple-element.59) | copy-start | bytes 2752516
  146.4 4.1 %copy-start.34 = (f32[3,1792]{1,0:T(4,128)S(1)}, f32[3,1792]{1,0:T(4,128)}, u32[]{:S(2)}) copy-start(f32[3,1792]{1,0:T(4,128)} %copy-done.33) | copy-start | bytes 64516
  155.2 6.2 %copy-start.17 = (f32[128,1536]{1,0:T(8,128)S(1)}, f32[128,1536]{1,0:T(8,128)}, u32[]{:S(2)}) copy-start(f32[128,1536]{1,0:T(8,128)} %get-tuple-element.70) | copy-start | bytes 2359300
  157.5 12.8 %collective-permute-start.1 = (f32[3,1792]{1,0:T(4,128)}, f32[3,1792]{1,0:T(4,128)}, u32[]{:S(2)}, u32[]{:S(2)}) collective-permute-start(f32[3,1792]{1,0:T(4,128)} %pad_add_fusion.1), channel_id=1, source_target_pairs={{1,0},{2,1},{3,2},{4,3},{5,4},{6,5},{7,6},{9,8},{10,9},{11,10},{12... | collective-permute-start | bytes 64520 | tf_op jit(solution)/shard_map/ppermute | solution.py:447
  159.0 5.2 %copy-start.27 = (f32[128,24]{1,0:T(8,128)S(1)}, f32[128,24]{1,0:T(8,128)}, u32[]{:S(2)}) copy-start(f32[128,24]{1,0:T(8,128)} %copy-done.26) | copy-start | bytes 36868
  159.0 5.2 %copy-start.59 = (f32[24]{0:T(128)S(1)}, f32[24]{0:T(128)}, u32[]{:S(2)}) copy-start(f32[24]{0:T(128)} %copy-done.58) | copy-start | bytes 292
  161.5 6.6 %copy-start.51 = (f32[1536]{0:T(1024)S(1)}, f32[1536]{0:T(1024)}, u32[]{:S(2)}) copy-start(f32[1536]{0:T(1024)} %multiply_reduce_fusion.6) | copy-start | bytes 18436
  161.5 6.8 %copy-start.29 = (f32[128,24]{0,1:T(8,128)S(1)}, f32[128,24]{0,1:T(8,128)}, u32[]{:S(2)}) copy-start(f32[128,24]{0,1:T(8,128)} %copy-done.28) | copy-start | bytes 36868
  161.5 7.0 %copy-start.50 = (f32[1792]{0:T(1024)S(1)}, f32[1792]{0:T(1024)}, u32[]{:S(2)}) copy-start(f32[1792]{0:T(1024)} %get-tuple-element.36) | copy-start | bytes 21508
  161.5 7.0 %copy-start.49 = (f32[1792]{0:T(1024)S(1)}, f32[1792]{0:T(1024)}, u32[]{:S(2)}) copy-start(f32[1792]{0:T(1024)} %get-tuple-element.37) | copy-start | bytes 21508
  161.5 7.0 %copy-start.48 = (f32[1792]{0:T(1024)S(1)}, f32[1792]{0:T(1024)}, u32[]{:S(2)}) copy-start(f32[1792]{0:T(1024)} %get-tuple-element.35) | copy-start | bytes 21508
  161.5 7.1 %copy-start.47 = (f32[1792]{0:T(1024)S(1)}, f32[1792]{0:T(1024)}, u32[]{:S(2)}) copy-start(f32[1792]{0:T(1024)} %get-tuple-element.41) | copy-start | bytes 21508
  161.5 7.1 %copy-start.23 = (f32[128,24]{1,0:T(8,128)S(1)}, f32[128,24]{1,0:T(8,128)}, u32[]{:S(2)}) copy-start(f32[128,24]{1,0:T(8,128)} %copy-done.22) | copy-start | bytes 36868
  161.5 7.1 %copy-start.25 = (f32[128,24]{1,0:T(8,128)S(1)}, f32[128,24]{1,0:T(8,128)}, u32[]{:S(2)}) copy-start(f32[128,24]{1,0:T(8,128)} %copy-done.24) | copy-start | bytes 36868
  161.5 7.1 %copy-start.61 = (f32[24]{0:T(128)S(1)}, f32[24]{0:T(128)}, u32[]{:S(2)}) copy-start(f32[24]{0:T(128)} %param.16) | copy-start | bytes 292
  161.5 7.1 %copy-start.63 = (f32[24]{0:T(128)S(1)}, f32[24]{0:T(128)}, u32[]{:S(2)}) copy-start(f32[24]{0:T(128)} %copy-done.62) | copy-start | bytes 292
  161.6 7.1 %copy-start.67 = (pred[128]{0:T(512)(128)(4,1)S(1)}, pred[128]{0:T(512)(128)(4,1)}, u32[]{:S(2)}) copy-start(pred[128]{0:T(512)(128)(4,1)} %iota_compare_fusion.3) | copy-start | bytes 388
  162.8 7.3 %copy-start.70 = (f32[24]{0:T(128)S(1)}, f32[24]{0:T(128)}, u32[]{:S(2)}) copy-start(f32[24]{0:T(128)} %param.17) | copy-start | bytes 292
  162.8 7.3 %copy-start.45 = (f32[1536]{0:T(1024)S(1)}, f32[1536]{0:T(1024)}, u32[]{:S(2)}) copy-start(f32[1536]{0:T(1024)} %get-tuple-element.48) | copy-start | bytes 18436
  162.8 7.5 %copy-start.14 = (f32[131,1792]{1,0:T(8,128)S(1)}, f32[131,1792]{1,0:T(8,128)}, u32[]{:S(2)}) copy-start(f32[131,1792]{1,0:T(8,128)} %pad_add_fusion) | copy-start | bytes 2817028
  166.7 5.7 %copy-start.5 = (bf16[128,768]{1,0:T(8,128)(2,1)S(1)}, bf16[128,768]{1,0:T(8,128)(2,1)}, u32[]{:S(2)}) copy-start(bf16[128,768]{1,0:T(8,128)(2,1)} %param.11) | copy-start | bytes 589828
  166.7 5.7 %copy-start.30 = (f32[768]{0:T(1024)S(1)}, f32[768]{0:T(1024)}, u32[]{:S(2)}) copy-start(f32[768]{0:T(1024)} %param.12) | copy-start | bytes 9220
  172.4 4.2 %copy-start.54 = (f32[128]{0:T(128)S(1)}, f32[128]{0:T(128)}, u32[]{:S(2)}) copy-start(f32[128]{0:T(128)} %copy-done.53) | copy-start | bytes 1540
  176.6 4.0 %copy-start.43 = (f32[1536]{0:T(1024)S(1)}, f32[1536]{0:T(1024)}, u32[]{:S(2)}) copy-start(f32[1536]{0:T(1024)} %get-tuple-element.38) | copy-start | bytes 18436
  176.6 4.0 %copy-start.44 = (f32[1792]{0:T(1024)S(1)}, f32[1792]{0:T(1024)}, u32[]{:S(2)}) copy-start(f32[1792]{0:T(1024)} %get-tuple-element.40) | copy-start | bytes 21508
  181.4 61.0 %copy-start.66 = (f32[128]{0:T(128)S(1)}, f32[128]{0:T(128)}, u32[]{:S(2)}) copy-start(f32[128]{0:T(128)} %copy-done.65) | copy-start | bytes 1540
  181.4 63.0 %copy-start.20 = (bf16[128,768]{1,0:T(8,128)(2,1)S(1)}, bf16[128,768]{1,0:T(8,128)(2,1)}, u32[]{:S(2)}) copy-start(bf16[128,768]{1,0:T(8,128)(2,1)} %param.21) | copy-start | bytes 589828
  (25 other events, 57.0 us)

commit v3 on v2

--- a/solution.py
+++ b/solution.py
@@ -60,14 +60,17 @@
     return (
         z_bits + x_bits + y_bits + core,
         z_bits + y_bits + x_bits + core,
-        x_bits + z_bits[:1] + y_bits + z_bits[1:] + core,
-        y_bits + z_bits[:1] + x_bits + z_bits[1:] + core,
-    )
-
-
-def split_lanes(width, count):
+        z_bits[:1] + x_bits + y_bits + z_bits[1:] + core,
+        z_bits[:1] + y_bits + x_bits + z_bits[1:] + core,
+    )
+
+
+SHARES = (0.3, 0.3, 0.2, 0.2)
+
+
+def split_lanes(width, shares):
     tiles = width // LANES
-    edges = [tiles * i // count * LANES for i in range(count + 1)]
+    edges = [round(tiles * sum(shares[:i])) * LANES for i in range(len(shares) + 1)]
     return [(low, high - low) for low, high in zip(edges, edges[1:])]
 
 
@@ -129,7 +132,7 @@
     streams = [
         (which, low, width, order)
         for which, shard in enumerate(shards)
-        for (low, width), order in zip(split_lanes(shard.shape[1], len(orders)), orders)
+        for (low, width), order in zip(split_lanes(shard.shape[1], SHARES), orders)
     ]
     return pl.pallas_call(
         partial(gather_kernel, seq_bits, streams, bits),
@@ -242,7 +245,7 @@
     streams = [
         (which, low, width, order)
         for which, term in enumerate(terms)
-        for (low, width), order in zip(split_lanes(term.shape[2], len(orders)), orders)
+        for (low, width), order in zip(split_lanes(term.shape[2], SHARES), orders)
     ]
     rows = terms[0].shape[1]
     in_vmem = pl.BlockSpec(memory_space=pltpu.VMEM)
@@ -459,8 +462,17 @@
     return jax.nn.silu(total)
 
 
+def head_lanes():
+    lanes = jnp.arange(DI, dtype=jnp.int32) // HEAD_DIM
+    return (jnp.arange(HEADS, dtype=jnp.int32)[:, None] == lanes[None, :]).astype(jnp.float32)
+
+
 def spread_heads(by_head):
-    return jnp.repeat(by_head, HEAD_DIM, axis=-1)
+    return jnp.dot(by_head, head_lanes(), precision=HIGH)
+
+
+def sum_heads(by_lane):
+    return jnp.dot(by_lane, head_lanes().T, precision=HIGH)
 
 
 def before_states(xbc, dt_raw, edge, conv_weight, conv_bias, dt_bias, a_log):
@@ -481,10 +493,7 @@
 
 
 def post_gate(ssd_out, xs, gate_part, skip_gain, gated_gain):
-    row_count = xs.shape[0]
-    skipped = (xs.reshape(row_count, HEADS, HEAD_DIM) * skip_gain[None, :, None]).reshape(
-        row_count, DI
-    )
+    skipped = xs * spread_heads(skip_gain[None, :])
     mixed_in = (ssd_out + skipped) * jax.nn.silu(gate_part)
     scale_rms = lax.rsqrt(jnp.mean(mixed_in * mixed_in, axis=-1, keepdims=True) + EPS)
     return mixed_in * scale_rms * gated_gain
@@ -535,7 +544,7 @@
     xs, scaled_x, b_mat, c_mat, cumulative, s_local = primal
     by_head = cumulative.T
     decay = jnp.exp(cumulative[-1])
-    wide_decay = spread_heads(decay)
+    wide_decay = spread_heads(decay[None, :])[0]
     square = (row_count, row_count)
     state_in, local_out = scan_states(
         s_local,
@@ -569,8 +578,8 @@
         collective_id=3,
     )
     c_cot = lax.dot_general(scaled_cot, state_in, (((1,), (1,)), ((), ())), precision=HIGH)
-    cum_cot = jnp.sum((ssd_cot * carried_part).reshape(row_count, HEADS, HEAD_DIM), axis=2)
-    last_cot = jnp.sum(later_grad * state_in, axis=0).reshape(HEADS, HEAD_DIM).sum(axis=1) * decay
+    cum_cot = sum_heads(ssd_cot * carried_part)
+    last_cot = sum_heads(jnp.sum(later_grad * state_in, axis=0, keepdims=True))[0] * decay
     is_last = (jnp.arange(row_count) == row_count - 1)[:, None]
     cum_cot = cum_cot + jnp.where(is_last, last_cot[None, :], 0.0)
     mid_grads = mid_back(

time: 250 us -> 231 us (0.924)
  local copies, waits for them, and re-layouts: 33.8 us -> 19.3 us
  Pallas kernels: 159 us -> 147 us
  matrix products: 32.8 us -> 40.7 us
  other arithmetic: 16.9 us -> 14.2 us
    dot_general x0 -> x9, matrix products: none -> 10.3 us  [the longest x8 8.46 us: spread_heads(): return jnp.dot(by_head, head_lanes(), precision=HIGH)]
    reshape x4 -> x0, local copies, waits for them, and re-layouts: 6.92 us -> none  [the longest x3 6.84 us: spread_heads(): return jnp.repeat(by_head, HEAD_DIM, axis=-1)]
    pallas_call x1, Pallas kernels: 56.4 us -> 49.8 us  [sum_to_owners(): pl.pallas_call(partial(sum_kernel, seq_bits, streams, bits, len(terms)),...]
    mul x5 -> x0, local copies, waits for them, and re-layouts: 5.86 us -> none  [the longest x1 2.38 us: body(): ssd_cot * carried_part]
    broadcast_in_dim x4 -> x0, local copies, waits for them, and re-layouts: 3.08 us -> none  [spread_heads(): return jnp.repeat(by_head, HEAD_DIM, axis=-1)]
    pallas_call x2, Pallas kernels: 51.5 us -> 48.5 us  [scan_states(): pl.pallas_call(partial(scan_kernel, count, reverse, work, len(given), len...]
    mul x2 -> x0, other arithmetic: 2.65 us -> none  [the longest x1 2.47 us: before_states(): fresh = jnp.dot(b_mat.T, scaled_x * spread_heads(tail), precision=HIGH)]
    dot_general x3, matrix products: 7.35 us -> 4.79 us  [before_states(): fresh = jnp.dot(b_mat.T, scaled_x * spread_heads(tail), precision=HIGH)]
  transfers between devices with their start and end apart: 2 -> 2, of which waited for: 0 -> 0; matrix products, arithmetic and copies ran while one was open for 10% -> 6% of each run, Pallas kernels for 0% -> 0%
where the time goes in v3:
time: 231 us; the launch traced here: 228 us
  Pallas kernels  147 us (64%)
  matrix products  40.7 us (18%)
  local copies, waits for them, and re-layouts  19.3 us (8%)
  other arithmetic  14.2 us (6%)
  starting transfers between devices  5.49 us (2%)
    pallas_call x1, Pallas kernels, sum_to_owners(): pl.pallas_call(partial(sum_kernel, seq_bits, streams, bits, len(terms)),...  49.8 us
    pallas_call x1, Pallas kernels, gather_all(): pl.pallas_call(partial(gather_kernel, seq_bits, streams, bits), out_shape...  49 us
    pallas_call x2, Pallas kernels, scan_states(): pl.pallas_call(partial(scan_kernel, count, reverse, work, len(given), len...  48.5 us
    dot_general x8, matrix products, spread_heads(): return jnp.dot(by_head, head_lanes(), precision=HIGH)  8.46 us
    unnamed x112, local copies, waits for them, and re-layouts  6.57 us
    dot_general x2, matrix products, contract_rows(): lax.dot_general(left, right, (((0,), (0,)), ((), ())), preferred_element_...  6.38 us
    slice x5, local copies, waits for them, and re-layouts, body(): parts.append(summed[at:at + a.size].reshape(a.shape))  6.03 us
    dot_general x2, matrix products, contract_cols(): lax.dot_general(left, right, (((1,), (1,)), ((), ())), preferred_element_...  5.83 us
  transfers between devices with their start and end apart: 2, of which 0 were waited for; matrix products, arithmetic and copies ran while one was open for 6% of the time, Pallas kernels for 0%

profile of v3, /device:TPU:0, one launch (start us, length us, event | category | flops | bytes accessed | tf_op | source)
XLA Modules:
  0.0 228.4 jit_solution(5562595109816479903)
XLA Ops:
  0.7 1.1 fusion.25
  2.2 1.6 pad.48.refs_0_
  3.8 49.0 %gather_rows.1 = (bf16[32,24,3456]{2,1,0:T(8,128)(2,1)}, bf16[32,24,1536]{2,1,0:T(8,128)(2,1)}) custom-call(bf16[24,3456]{1,0:T(8,128)(2,1)} %pad.48.refs_0_, bf16[24,1536]{1,0:T(8,128)(2,1)} %refs_1_.1), custom_call_target="tpu_custom_call" | custom-call | tf_op jit(solution)/shard_map/gather_rows/pallas_call | solution.py:137
  52.9 3.6 %fusion.51 = f32[128,3456]{1,0:T(8,128)S(1)} fusion(bf16[768,3456]{1,0:T(8,128)(2,1)} %bitcast.56, bf16[128,768]{1,0:T(8,128)(2,1)} %param.11, f32[768]{0:T(1024)} %param.12, f32[128]{0:T(128)S(1)} %fusion.60), kind=kOutput, calls=%fused_computation.109 | convolution fusion | flops 679870464 | bytes 7278080 | tf_op jit(solution)/shard_map/dot_general | solution.py:536
  56.5 3.9 %collective-permute-start = (f32[3,1792]{1,0:T(4,128)S(1)}, f32[3,1792]{1,0:T(4,128)S(1)}, u32[]{:S(2)}, u32[]{:S(2)}) collective-permute-start(f32[3,1792]{1,0:T(4,128)S(1)} %slice.107), channel_id=1, source_target_pairs={{0,1},{1,2},{2,3},{3,4},{4,5},{5,6},{6,7},{8,9},{9,10},{10,11},{11... | collective-permute-start | bytes 64520 | tf_op jit(solution)/shard_map/ppermute | solution.py:450
  61.4 1.4 fusion.30
  62.7 0.8 convolution_reduce_fusion
  63.5 0.7 slice_reduce_fusion.4
  64.2 0.8 fusion.31.refs_1_
  65.5 1.0 slice.108
  67.2 4.0 %fusion.11 = (f32[128,1792]{1,0:T(8,128)S(1)}, f32[128,1792]{1,0:T(8,128)}) fusion(f32[128,1792]{1,0:T(8,128)} %slice.108, f32[1792]{0:T(1024)} %get-tuple-element.46, f32[3,1792]{1,0:T(4,128)} %copy-done.30, f32[1792]{0:T(1024)} %get-tuple-element.47, f32[1792]{0:T(1024)} %get-tuple-element.45, f32[1792]{0:T(1024)} %get-tuple-element.44, f32[1792]{0:T(1024)} %param.15), kind=kLoop, calls=%fused_computation.41 | loop fusion | flops 3440640 | bytes 2809856 | tf_op jit(solution)/shard_map/jvp(jit(silu))/mul | solution.py:462
  71.2 0.7 fusion.71
  71.8 1.6 fusion.70
  73.5 0.9 copy-done.12
  74.4 1.6 convolution_convert_fusion.3
  76.0 24.7 %scan_states.1 = (bf16[8,16,1536]{2,1,0:T(8,128)(2,1)}, f32[128,1536]{1,0:T(8,128)}) custom-call(bf16[8,16,1536]{2,1,0:T(8,128)(2,1)} %bitcast.66, f32[1,1536]{1,0:T(1,128)} %fusion.31.refs_1_, f32[128,1536]{1,0:T(8,128)} %get-tuple-element.55.refs_2_.refs_3_, f32[128,128]{1,0:T(8,128)} %get-tuple-element.64.refs_3_.refs_4_, ...), custom_call_target="tpu_custom_call" | custom-call | tf_op jit(solution)/shard_map/scan_states/pallas_call | solution.py:426
  100.7 3.4 %multiply_reduce_fusion.8 = (f32[128]{0:T(128)S(1)}, f32[128,1536]{1,0:T(8,128)S(1)}, f32[128,1536]{1,0:T(8,128)S(1)}, f32[128,1536]{1,0:T(8,128)}) fusion(f32[128,3456]{1,0:T(8,128)S(1)} %fusion.51, f32[1536]{0:T(1024)S(1)} %copy-done.45, f32[128,1792]{1,0:T(8,128)S(1)} %get-tuple-element.56, f32[128,1536]{1,0:T(8,128)} %get-tuple-element.24, ...), kind=kOutput, calls=%fused_computation.56 | convolution fusion | flops 304152448 | bytes 5972480 | tf_op jit(solution)/shard_map/dot_general | solution.py:560
  104.1 1.6 fusion
  105.7 1.1 multiply_reduce_fusion.5
  106.9 3.2 %multiply_reduce_fusion.4 = (f32[1536]{0:T(1024)}, f32[128,1536]{1,0:T(8,128)S(1)}, bf16[128,1536]{1,0:T(8,128)(2,1)}) fusion(f32[128,1792]{1,0:T(8,128)S(1)} %get-tuple-element.56, f32[128,3456]{1,0:T(8,128)} %copy-done.4, f32[128,1536]{1,0:T(8,128)S(1)} %get-tuple-element.52, f32[128]{0:T(128)S(1)} %multiply_multiply_fusion.1, f32[128]{0:T(128)S(1)} %fusion.61, ...), kind=kLoop, calls=%fused_computation.46 | loop fusion | flops 3930624 | bytes 5125120 | tf_op jit(solution)/shard_map/transpose(jvp())/reduce_sum | solution.py:496
  110.1 1.6 convolution_convert_fusion.2
  111.7 23.8 %scan_back.1 = (bf16[8,16,1536]{2,1,0:T(8,128)(2,1)}, f32[128,1536]{1,0:T(8,128)}, f32[128,128]{1,0:T(8,128)}, f32[128,128]{1,0:T(8,128)}, f32[24,128]{1,0:T(8,128)}) custom-call(bf16[8,16,1536]{2,1,0:T(8,128)(2,1)} %bitcast.65, f32[1,1536]{1,0:T(1,128)} %fusion.31.refs_1_, f32[128,1536]{1,0:T(8,128)} %copy-done.1, ...), custom_call_target="tpu_custom_call" | custom-call | tf_op jit(solution)/shard_map/scan_back/pallas_call | solution.py:426
  135.5 2.1 convolution_add_fusion.4
  137.7 1.6 convolution_add_fusion.3
  139.4 1.6 multiply_add_fusion.1
  141.6 1.4 multiply_reduce_fusion.2
  143.3 1.2 pad_add_fusion
  145.7 2.4 %convolution_convert_fusion.1 = bf16[1536,768]{0,1:T(8,128)(2,1)} fusion(bf16[128,768]{1,0:T(8,128)(2,1)S(1)} %copy-done.22, f32[128,1536]{1,0:T(8,128)S(1)} %get-tuple-element.52, f32[1536]{0:T(1024)S(1)} %copy-done.29, f32[128]{0:T(128)S(1)} %fusion.61), kind=kOutput, calls=%fused_computation.1 | convolution fusion | flops 303759360 | bytes 3348992 | tf_op jit(solution)/shard_map/dot_general | solution.py:503
  148.1 1.6 collective-permute-start.1
  149.8 0.7 copy.31
  150.5 1.8 fusion.74
  152.7 1.8 fusion.3
  154.5 1.1 multiply_reduce_fusion.9
  155.7 1.5 fusion.72
  157.6 0.8 fusion.10
  158.8 4.2 %fusion.23 = (f32[768]{0:T(1024)S(1)}, f32[128]{0:T(128)S(1)}, f32[128,768]{1,0:T(8,128)S(1)}) fusion(bf16[128,768]{1,0:T(8,128)(2,1)S(1)} %copy-done.8, f32[128]{0:T(128)S(1)} %fusion.60, f32[768]{0:T(1024)S(1)} %copy-done.28, bf16[128,3456]{1,0:T(8,128)(2,1)S(1)} %concatenate.11, bf16[768,3456]{1,0:T(8,128)(2,1)} %bitcast.57), kind=kOutput, calls=%fused_computation.74 | convolution fusion | flops 680164480 | bytes 6790144 | tf_op jit(solution)/shard_map/dot_general | solution.py:509
  163.0 4.0 %convolution_convert_fusion = bf16[768,3456]{1,0:T(8,128)(2,1)} fusion(bf16[128,3456]{1,0:T(8,128)(2,1)S(1)} %concatenate.11, bf16[128,768]{1,0:T(8,128)(2,1)S(1)} %copy-done.8, f32[768]{0:T(1024)S(1)} %copy-done.28, f32[128]{0:T(128)S(1)} %fusion.60), kind=kOutput, calls=%fused_computation | convolution fusion | flops 682524672 | bytes 6393344 | tf_op jit(solution)/shard_map/dot_general | solution.py:503
  167.1 0.6 pad_bitcast_fusion.refs_2_
  167.7 49.8 %sum_rows.1 = (f32[24,3456]{1,0:T(8,128)}, f32[24,1536]{1,0:T(8,128)}, f32[96,128]{1,0:T(8,128)}) custom-call(bf16[32,24,3456]{2,1,0:T(8,128)(2,1)} %bitcast.55, bf16[32,24,1536]{2,1,0:T(8,128)(2,1)} %bitcast.60, f32[96,128]{1,0:T(8,128)} %pad_bitcast_fusion.refs_2_), custom_call_target="tpu_custom_call" | custom-call | tf_op jit(solution)/shard_map/sum_rows/pallas_call | solution.py:257
  217.5 1.3 slice_bitcast_fusion.2
  218.8 0.8 slice.99
  219.5 1.3 slice_bitcast_fusion.1
  220.8 1.3 slice_bitcast_fusion
  222.2 0.6 reshape.187
  222.8 1.4 fusion.73
  224.2 0.9 fusion.24
  225.1 1.7 copy.41
  226.8 1.6 copy.42
  (140 shorter events, 5.9 us)
Async XLA Ops:
  0.6 62.1 %copy-start = (f32[24]{0:T(128)S(1)}, f32[24]{0:T(128)}, u32[]{:S(2)}) copy-start(f32[24]{0:T(128)} %param.18) | copy-start | bytes 292
  52.8 7.5 %copy-start.53 = (f32[24]{0:T(128)S(1)}, f32[24]{0:T(128)}, u32[]{:S(2)}) copy-start(f32[24]{0:T(128)} %param.17) | copy-start | bytes 292
  52.9 7.5 %copy-start.49 = (f32[24]{0:T(128)S(1)}, f32[24]{0:T(128)}, u32[]{:S(2)}) copy-start(f32[24]{0:T(128)} %param.16) | copy-start | bytes 292
  52.9 10.7 %copy-start.43 = (f32[1792,4]{0,1:T(4,128)S(1)}, f32[1792,4]{0,1:T(4,128)}, u32[]{:S(2)}) copy-start(f32[1792,4]{0,1:T(4,128)} %param.14) | copy-start | bytes 86020
  56.5 44.2 %copy-start.4 = (f32[128,3456]{1,0:T(8,128)}, f32[128,3456]{1,0:T(8,128)S(1)}, u32[]{:S(2)}) copy-start(f32[128,3456]{1,0:T(8,128)S(1)} %fusion.51) | copy-start | bytes 5308420
  56.5 10.1 %collective-permute-start = (f32[3,1792]{1,0:T(4,128)S(1)}, f32[3,1792]{1,0:T(4,128)S(1)}, u32[]{:S(2)}, u32[]{:S(2)}) collective-permute-start(f32[3,1792]{1,0:T(4,128)S(1)} %slice.107), channel_id=1, source_target_pairs={{0,1},{1,2},{2,3},{3,4},{4,5},{5,6},{6,7},{8,9},{9,10},{10,11},{11... | collective-permute-start | bytes 64520 | tf_op jit(solution)/shard_map/ppermute | solution.py:450
  60.4 5.1 %copy-start.52 = (f32[24]{0:T(128)}, f32[24]{0:T(128)S(1)}, u32[]{:S(2)}) copy-start(f32[24]{0:T(128)S(1)} %exponential_negate_fusion) | copy-start | bytes 292
  60.9 10.9 %copy-start.10 = (f32[128,1536]{1,0:T(8,128)}, f32[128,1536]{1,0:T(8,128)S(1)}, u32[]{:S(2)}) copy-start(f32[128,1536]{1,0:T(8,128)S(1)} %fusion.33) | copy-start | bytes 2359300
  61.1 5.5 %copy-start.26 = (f32[128,24]{0,1:T(8,128)}, f32[128,24]{0,1:T(8,128)S(1)}, u32[]{:S(2)}) copy-start(f32[128,24]{0,1:T(8,128)S(1)} %fusion.47) | copy-start | bytes 36868
  61.3 4.1 %copy-start.46 = (f32[24]{0:T(128)}, f32[24]{0:T(128)S(1)}, u32[]{:S(2)}) copy-start(f32[24]{0:T(128)S(1)} %slice_reduce_fusion) | copy-start | bytes 292
  66.6 5.2 %copy-start.47 = (f32[24]{0:T(128)S(1)}, f32[24]{0:T(128)}, u32[]{:S(2)}) copy-start(f32[24]{0:T(128)} %copy-done.46) | copy-start | bytes 292
  71.8 28.9 %copy-start.45 = (f32[1536]{0:T(1024)S(1)}, f32[1536]{0:T(1024)}, u32[]{:S(2)}) copy-start(f32[1536]{0:T(1024)} %convolution_reduce_fusion) | copy-start | bytes 18436
  100.7 3.4 %copy-start.6 = (bf16[32,24,1536]{2,1,0:T(8,128)(2,1)S(1)}, bf16[32,24,1536]{2,1,0:T(8,128)(2,1)}, u32[]{:S(2)}) copy-start(bf16[32,24,1536]{2,1,0:T(8,128)(2,1)} %get-tuple-element.26) | copy-start | bytes 7077892
  100.7 3.4 %copy-start.7 = (bf16[128,768]{1,0:T(8,128)(2,1)S(1)}, bf16[128,768]{1,0:T(8,128)(2,1)}, u32[]{:S(2)}) copy-start(bf16[128,768]{1,0:T(8,128)(2,1)} %param.11) | copy-start | bytes 589828
  100.7 3.4 %copy-start.29 = (f32[1536]{0:T(1024)S(1)}, f32[1536]{0:T(1024)}, u32[]{:S(2)}) copy-start(f32[1536]{0:T(1024)} %param.19) | copy-start | bytes 18436
  106.9 3.2 %copy-start.16 = (f32[128,1536]{1,0:T(8,128)S(1)}, f32[128,1536]{1,0:T(8,128)}, u32[]{:S(2)}) copy-start(f32[128,1536]{1,0:T(8,128)} %fusion.30) | copy-start | bytes 2359300
  111.7 27.6 %copy-start.11 = (f32[128,1536]{1,0:T(8,128)S(1)}, f32[128,1536]{1,0:T(8,128)}, u32[]{:S(2)}) copy-start(f32[128,1536]{1,0:T(8,128)} %copy-done.10) | copy-start | bytes 2359300
  135.5 2.2 copy-start.19
  135.5 3.8 %copy-start.2 = (f32[128,1536]{1,0:T(8,128)S(1)}, f32[128,1536]{1,0:T(8,128)}, u32[]{:S(2)}) copy-start(f32[128,1536]{1,0:T(8,128)} %copy-done.1) | copy-start | bytes 2359300
  135.5 3.8 %copy-start.13 = (f32[128,1536]{1,0:T(8,128)S(1)}, f32[128,1536]{1,0:T(8,128)}, u32[]{:S(2)}) copy-start(f32[128,1536]{1,0:T(8,128)} %get-tuple-element.70) | copy-start | bytes 2359300
  135.5 3.8 %copy-start.20 = (f32[128,1536]{1,0:T(8,128)S(1)}, f32[128,1536]{1,0:T(8,128)}, u32[]{:S(2)}) copy-start(f32[128,1536]{1,0:T(8,128)} %get-tuple-element.30) | copy-start | bytes 2359300
  139.3 1.9 copy-start.9
  139.4 2.3 copy-start.18
  139.4 2.2 copy-start.31
  140.9 2.1 copy-start.32
  140.9 2.1 copy-start.33
  140.9 2.1 copy-start.34
  140.9 2.1 copy-start.35
  145.6 4.2 %copy-start.44 = (f32[24,128]{1,0:T(8,128)S(1)}, f32[24,128]{1,0:T(8,128)}, u32[]{:S(2)}) copy-start(f32[24,128]{1,0:T(8,128)} %get-tuple-element.31) | copy-start | bytes 36868
  145.6 4.9 %copy-start.3 = (f32[128,1536]{1,0:T(8,128)S(1)}, f32[128,1536]{1,0:T(8,128)}, u32[]{:S(2)}) copy-start(f32[128,1536]{1,0:T(8,128)} %get-tuple-element.55.refs_2_.refs_3_) | copy-start | bytes 2359300
  145.6 4.9 %copy-start.48 = (f32[24]{0:T(128)S(1)}, f32[24]{0:T(128)}, u32[]{:S(2)}) copy-start(f32[24]{0:T(128)} %copy-done.46) | copy-start | bytes 292
  145.7 6.6 %copy-start.27 = (f32[128,24]{0,1:T(8,128)S(1)}, f32[128,24]{0,1:T(8,128)}, u32[]{:S(2)}) copy-start(f32[128,24]{0,1:T(8,128)} %copy-done.26) | copy-start | bytes 36868
  148.1 7.5 %copy-start.14 = (f32[128,1536]{1,0:T(8,128)S(1)}, f32[128,1536]{1,0:T(8,128)}, u32[]{:S(2)}) copy-start(f32[128,1536]{1,0:T(8,128)} %get-tuple-element.70) | copy-start | bytes 2359300
  148.1 9.5 %collective-permute-start.1 = (f32[3,1792]{1,0:T(4,128)}, f32[3,1792]{1,0:T(4,128)}, u32[]{:S(2)}, u32[]{:S(2)}) collective-permute-start(f32[3,1792]{1,0:T(4,128)} %pad_add_fusion.1), channel_id=1, source_target_pairs={{1,0},{2,1},{3,2},{4,3},{5,4},{6,5},{7,6},{9,8},{10,9},{11,10},{12... | collective-permute-start | bytes 64520 | tf_op jit(solution)/shard_map/ppermute | solution.py:450
  150.5 5.1 %copy-start.15 = (f32[128,1536]{1,0:T(8,128)S(1)}, f32[128,1536]{1,0:T(8,128)}, u32[]{:S(2)}) copy-start(f32[128,1536]{1,0:T(8,128)} %get-tuple-element.74) | copy-start | bytes 2359300
  150.5 5.2 %copy-start.21 = (f32[128,1536]{1,0:T(8,128)S(1)}, f32[128,1536]{1,0:T(8,128)}, u32[]{:S(2)}) copy-start(f32[128,1536]{1,0:T(8,128)} %get-tuple-element.30) | copy-start | bytes 2359300
  152.6 4.6 %copy-start.42 = (f32[1792]{0:T(1024)S(1)}, f32[1792]{0:T(1024)}, u32[]{:S(2)}) copy-start(f32[1792]{0:T(1024)} %get-tuple-element.36) | copy-start | bytes 21508
  152.6 4.6 %copy-start.41 = (f32[1792]{0:T(1024)S(1)}, f32[1792]{0:T(1024)}, u32[]{:S(2)}) copy-start(f32[1792]{0:T(1024)} %get-tuple-element.37) | copy-start | bytes 21508
  152.7 4.6 %copy-start.40 = (f32[1792]{0:T(1024)S(1)}, f32[1792]{0:T(1024)}, u32[]{:S(2)}) copy-start(f32[1792]{0:T(1024)} %get-tuple-element.35) | copy-start | bytes 21508
  152.7 4.6 %copy-start.39 = (f32[1792]{0:T(1024)S(1)}, f32[1792]{0:T(1024)}, u32[]{:S(2)}) copy-start(f32[1792]{0:T(1024)} %get-tuple-element.41) | copy-start | bytes 21508
  152.7 4.6 %copy-start.54 = (f32[24]{0:T(128)S(1)}, f32[24]{0:T(128)}, u32[]{:S(2)}) copy-start(f32[24]{0:T(128)} %param.17) | copy-start | bytes 292
  152.7 4.6 %copy-start.38 = (f32[1536]{0:T(1024)S(1)}, f32[1536]{0:T(1024)}, u32[]{:S(2)}) copy-start(f32[1536]{0:T(1024)} %get-tuple-element.48) | copy-start | bytes 18436
  152.7 4.9 %copy-start.17 = (f32[131,1792]{1,0:T(8,128)S(1)}, f32[131,1792]{1,0:T(8,128)}, u32[]{:S(2)}) copy-start(f32[131,1792]{1,0:T(8,128)} %pad_add_fusion) | copy-start | bytes 2817028
  155.7 2.8 %copy-start.24 = (bf16[128,1536]{1,0:T(8,128)(2,1)S(1)}, bf16[128,1536]{1,0:T(8,128)(2,1)}, u32[]{:S(2)}) copy-start(bf16[128,1536]{1,0:T(8,128)(2,1)} %get-tuple-element.58) | copy-start | bytes 1179652
  163.0 4.0 %copy-start.36 = (f32[1536]{0:T(1024)S(1)}, f32[1536]{0:T(1024)}, u32[]{:S(2)}) copy-start(f32[1536]{0:T(1024)} %get-tuple-element.38) | copy-start | bytes 18436
  163.0 4.0 %copy-start.37 = (f32[1792]{0:T(1024)S(1)}, f32[1792]{0:T(1024)}, u32[]{:S(2)}) copy-start(f32[1792]{0:T(1024)} %get-tuple-element.40) | copy-start | bytes 21508
  167.7 54.4 %copy-start.51 = (f32[128]{0:T(128)S(1)}, f32[128]{0:T(128)}, u32[]{:S(2)}) copy-start(f32[128]{0:T(128)} %copy-done.50) | copy-start | bytes 1540
  167.7 56.5 %copy-start.23 = (bf16[128,768]{1,0:T(8,128)(2,1)S(1)}, bf16[128,768]{1,0:T(8,128)(2,1)}, u32[]{:S(2)}) copy-start(bf16[128,768]{1,0:T(8,128)(2,1)} %param.21) | copy-start | bytes 589828
  (9 other events, 11.1 us)
